TPU v7x, 32 devices: a whole 2x2x4 slice. The times are simulated.
32 devices in a mesh: grp: 2 (over core), tile: 16 (over z, y, x).
Axes of the slice: x: 2, y: 2, z: 4, core: 2. Of those that a mesh axis runs over, the one named last changes fastest.
Arguments:
- right_side: float32 [64, 8192], P('grp', 'tile'), may hold values from -8 to 8
- diagonal: float32 [64, 8192], P('grp', 'tile'), may hold values from 0.25 to 2
- inverse_factor: float32 [2048, 2048], P(('grp', 'tile')), may hold values from -2 to 2, as said below
Outputs:
- solution_field: float32 [64, 8192], P('grp', 'tile')
Inputs may be any that keep to these rules, and one draw needn't show every extreme that they name: `inverse_factor`: zero above the diagonal; the diagonal lies between 1 and 2.
All inputs are finite; a program needn't handle non-finite values.
Results may differ from a plain program's by a relative error of at most 0.0003.
Values sent between devices are 32-bit elements; how exact they have to be, the bound alone decides.
No kernel may reach another device: no remote copies, remote signals or barrier semaphores. Data moves between devices by JAX's collectives and lax.ppermute only.
A program may use at most 64 MiB of HBM per device.

v0:
```python
import jax
import jax.numpy as jnp
from jax import lax
from jax.sharding import PartitionSpec as P

FAC = 16
SWEEPS = 4
CYCLES = 2


def extended(block, sides, width):
    for axis, dim in sides:
        count = lax.axis_size(axis)
        forward = [(i, i + 1) for i in range(count - 1)]
        backward = [(target, source) for source, target in forward]
        low = lax.ppermute(
            lax.slice_in_dim(block, block.shape[dim] - width, None, axis=dim), axis, forward
        )
        high = lax.ppermute(lax.slice_in_dim(block, 0, width, axis=dim), axis, backward)
        block = jnp.concatenate([low, block, high], axis=dim)
    return block


def crop_margin(array, depth):
    return array[depth : array.shape[0] - depth, depth : array.shape[1] - depth]


def apply_inner(field, diag_part):
    beside = field[2:, 1:-1] + field[:-2, 1:-1] + field[1:-1, 2:] + field[1:-1, :-2]
    beside = beside + field[2:, :-2] + field[:-2, 2:]
    return (6.0 + diag_part) * field[1:-1, 1:-1] - beside


def shards(right_side, diagonal, inverse_factor):
    rows_here, cols_here = right_side.shape
    coarse_here = inverse_factor.shape[0]
    solution_field = jnp.zeros_like(right_side)
    width = SWEEPS
    stacked = jnp.stack([right_side, diagonal], axis=0)
    padded_both = extended(stacked, (("grp", 1), ("tile", 2)), width)
    pad_rhs = padded_both[0]
    pad_diag = padded_both[1]
    row_glob = (
        lax.axis_index("grp") * rows_here
        - width
        + jnp.arange(rows_here + 2 * width, dtype=jnp.int32)
    )
    col_glob = (
        lax.axis_index("tile") * cols_here
        - width
        + jnp.arange(cols_here + 2 * width, dtype=jnp.int32)
    )
    row_ok = (row_glob >= 0) & (row_glob < rows_here * lax.axis_size("grp"))
    col_ok = (col_glob >= 0) & (col_glob < cols_here * lax.axis_size("tile"))
    inside = (row_ok[:, None] & col_ok[None, :]).astype(jnp.float32)
    for cycle in range(CYCLES):
        if cycle == 0:
            wide_res = crop_margin(pad_rhs, 1) * crop_margin(inside, 1)
        else:
            pad_sol = extended(solution_field, (("grp", 0), ("tile", 1)), width)
            wide_res = (
                crop_margin(pad_rhs, 1) - apply_inner(pad_sol, crop_margin(pad_diag, 1))
            ) * crop_margin(inside, 1)
        margin = width - 1
        wide_smooth = 0.8 * wide_res / (6.0 + crop_margin(pad_diag, 1))
        for sweep in range(SWEEPS - 1):
            lower = margin - 1
            diag_low = crop_margin(pad_diag, width - lower)
            res_low = crop_margin(wide_res, width - 1 - lower)
            update = (res_low - apply_inner(wide_smooth, diag_low)) / (6.0 + diag_low)
            wide_smooth = (crop_margin(wide_smooth, 1) + 0.8 * update) * crop_margin(
                inside, width - lower
            )
            margin = lower
        smoothed = crop_margin(wide_smooth, margin)
        residual = crop_margin(wide_res, width - 1)
        coarse_rhs = jnp.mean(
            residual.reshape(rows_here // FAC, FAC, cols_here // FAC, FAC), axis=(1, 3)
        ).reshape(-1)
        inner = jnp.dot(
            inverse_factor,
            lax.all_gather(coarse_rhs, ("grp", "tile"), axis=0, tiled=True),
            precision=lax.Precision.HIGHEST,
        )
        whole_term = jnp.dot(inner, inverse_factor, precision=lax.Precision.HIGHEST)
        summed = lax.psum(whole_term, ("grp", "tile"))
        offset = lax.axis_index(("grp", "tile")) * coarse_here
        coarse_fix = lax.dynamic_slice_in_dim(summed, offset, coarse_here, 0)
        blocks = coarse_fix.reshape(rows_here // FAC, 1, cols_here // FAC, 1)
        spread_fix = jnp.broadcast_to(
            blocks, (rows_here // FAC, FAC, cols_here // FAC, FAC)
        ).reshape(rows_here, cols_here)
        solution_field = solution_field + smoothed + 0.5 * spread_fix
    return solution_field


def solution(mesh):
    placed = (P("grp", "tile"), P("grp", "tile"), P(("grp", "tile"), None))
    return jax.shard_map(
        shards, mesh=mesh, in_specs=placed, out_specs=P("grp", "tile"), check_vma=False
    )
```

profile of v0, /device:TPU:0, one launch (start us, length us, event | category | flops | bytes accessed | tf_op | source)
XLA Modules:
  0.0 199.8 jit_solution(2719538963954903528)
XLA Ops:
  0.0 0.0 copy-start
  0.0 0.0 copy-start.1
  0.0 0.0 copy-start.2
  0.0 0.8 pad_maximum_fusion.10
  0.8 2.4 %collective-permute-start = (f32[2,4,512]{2,1,0:T(4,128)S(1)}, f32[2,4,512]{2,1,0:T(4,128)S(1)}, u32[]{:S(2)}, u32[]{:S(2)}) collective-permute-start(f32[2,4,512]{2,1,0:T(4,128)S(1)} %get-tuple-element.13), channel_id=1, source_target_pairs={{0,16},{1,17},{2,18},{3,19},{4,20},{5,21},{6,22},{7,23},{8,24},{9,... | collective-permute-start | bytes 49160 | tf_op jit(solution)/shard_map/ppermute | solution.py:16
  3.2 1.3 collective-permute-start.1
  4.6 0.0 collective-permute-done
  4.6 1.7 collective-permute-done.1
  6.3 0.0 copy-done.1
  6.3 0.0 copy-done.2
  6.3 0.1 pad_maximum_fusion.5
  6.4 4.2 %collective-permute-start.2 = (f32[2,40,4]{2,1,0:T(8,128)S(1)}, f32[2,40,4]{2,1,0:T(8,128)S(1)}, u32[]{:S(2)}, u32[]{:S(2)}) collective-permute-start(f32[2,40,4]{2,1,0:T(8,128)S(1)} %get-tuple-element.11), channel_id=1, source_target_pairs={{0,1},{1,2},{2,3},{3,4},{4,5},{5,6},{6,7},{7,8},{8,9},{9,10},{10,1... | collective-permute-start | bytes 3848 | tf_op jit(solution)/shard_map/ppermute | solution.py:16
  10.6 1.3 collective-permute-start.3
  11.9 0.1 and_convert_fusion
  12.0 0.3 collective-permute-done.2
  12.3 4.2 %collective-permute-done.3 = f32[2,40,4]{2,1,0:T(8,128)S(1)} collective-permute-done((f32[2,40,4]{2,1,0:T(8,128)S(1)}, f32[2,40,4]{2,1,0:T(8,128)S(1)}, u32[]{:S(2)}, u32[]{:S(2)}) %collective-permute-start.3) | collective-permute-done | bytes 1312 | tf_op jit(solution)/shard_map/ppermute | solution.py:19
  16.5 0.2 pad_maximum_fusion
  16.7 0.2 multiply_divide_fusion.1
  16.9 0.1 slice.340
  17.0 0.3 fusion.26
  17.3 0.3 fusion.20
  17.5 0.2 reshape.42
  17.8 0.1 reduce_sum.18
  17.9 0.1 reshape.44
  18.0 0.2 dynamic-update-slice
  18.2 42.4 %all-reduce = f32[2048]{0:T(1024)S(1)} all-reduce(f32[2048]{0:T(1024)S(1)} %dynamic-update-slice), channel_id=1, replica_groups=mesh['grp'=2,'tile'=16] {'grp','tile'}, use_global_device_ids=true, to_apply=%add | all-reduce | flops 2048 | bytes 16384
  60.5 0.0 copy-done
  60.5 0.5 convolution_bitcast_fusion.1
  61.0 0.4 fusion.47
  61.4 39.1 %psum.14 = f32[2048]{0:T(1024)S(1)} all-reduce(f32[2048]{0:T(1024)S(1)} %bitcast.35), channel_id=1, replica_groups=mesh['grp'=2,'tile'=16] {'grp','tile'}, use_global_device_ids=true, to_apply=%region_1.0 | all-reduce | flops 2048 | bytes 16384 | tf_op jit(solution)/shard_map/psum | solution.py:86
  100.6 0.1 dynamic-slice_multiply_fusion.1
  100.6 0.1 mul.119
  100.7 0.1 broadcast_in_dim.4
  100.8 0.3 mul.120
  101.1 0.2 fusion.41
  101.3 1.3 collective-permute-start.4
  102.6 1.3 collective-permute-start.5
  103.9 0.0 collective-permute-done.4
  104.0 1.8 collective-permute-done.5
  105.7 0.1 pad_maximum_fusion.8
  105.8 4.2 %collective-permute-start.6 = (f32[40,4]{1,0:T(8,128)S(1)}, f32[40,4]{1,0:T(8,128)S(1)}, u32[]{:S(2)}, u32[]{:S(2)}) collective-permute-start(f32[40,4]{1,0:T(8,128)S(1)} %get-tuple-element.15), channel_id=1, source_target_pairs={{0,1},{1,2},{2,3},{3,4},{4,5},{5,6},{6,7},{7,8},{8,9},{9,10},{10,1... | collective-permute-start | bytes 1928 | tf_op jit(solution)/shard_map/ppermute | solution.py:16
  110.0 1.3 collective-permute-start.7
  111.3 0.2 collective-permute-done.6
  111.4 4.2 %collective-permute-done.7 = f32[40,4]{1,0:T(8,128)S(1)} collective-permute-done((f32[40,4]{1,0:T(8,128)S(1)}, f32[40,4]{1,0:T(8,128)S(1)}, u32[]{:S(2)}, u32[]{:S(2)}) %collective-permute-start.7) | collective-permute-done | bytes 672 | tf_op jit(solution)/shard_map/ppermute | solution.py:19
  115.6 0.1 pad_maximum_fusion.1
  115.8 0.3 multiply_divide_fusion
  116.1 0.1 slice.375
  116.1 0.3 fusion.11
  116.4 0.3 fusion.5
  116.7 0.2 reshape.43
  116.9 0.1 reduce_sum.19
  117.1 0.1 reshape.46
  117.2 0.2 dynamic-update-slice.1
  117.4 40.5 %all-reduce.1 = f32[2048]{0:T(1024)S(1)} all-reduce(f32[2048]{0:T(1024)S(1)} %dynamic-update-slice.1), channel_id=1, replica_groups=mesh['grp'=2,'tile'=16] {'grp','tile'}, use_global_device_ids=true, to_apply=%add.1 | all-reduce | flops 2048 | bytes 16384
  157.9 0.5 convolution_bitcast_fusion
  158.4 0.4 fusion.48
  158.8 39.6 %psum.15 = f32[2048]{0:T(1024)S(1)} all-reduce(f32[2048]{0:T(1024)S(1)} %bitcast.37), channel_id=1, replica_groups=mesh['grp'=2,'tile'=16] {'grp','tile'}, use_global_device_ids=true, to_apply=%region_3.0 | all-reduce | flops 2048 | bytes 16384 | tf_op jit(solution)/shard_map/psum | solution.py:86
  198.4 0.1 dynamic-slice_multiply_fusion
  198.5 0.1 mul.134
  198.5 0.1 broadcast_in_dim.5
  198.7 0.3 mul.135
  198.9 0.8 fusion.34
  (8 shorter events, 0.1 us)
Async XLA Ops:
  0.0 60.5 %copy-start = (f32[64,2048]{1,0:T(8,128)S(1)}, f32[64,2048]{1,0:T(8,128)}, u32[]{:S(2)}) copy-start(f32[64,2048]{1,0:T(8,128)} %param.5) | copy-start | bytes 1572868
  0.0 6.3 %copy-start.1 = (f32[32,512]{1,0:T(8,128)S(1)}, f32[32,512]{1,0:T(8,128)}, u32[]{:S(2)}) copy-start(f32[32,512]{1,0:T(8,128)} %param.4) | copy-start | bytes 196612
  0.0 6.3 %copy-start.2 = (f32[32,512]{1,0:T(8,128)S(1)}, f32[32,512]{1,0:T(8,128)}, u32[]{:S(2)}) copy-start(f32[32,512]{1,0:T(8,128)} %param.3) | copy-start | bytes 196612
  0.8 3.7 %collective-permute-start = (f32[2,4,512]{2,1,0:T(4,128)S(1)}, f32[2,4,512]{2,1,0:T(4,128)S(1)}, u32[]{:S(2)}, u32[]{:S(2)}) collective-permute-start(f32[2,4,512]{2,1,0:T(4,128)S(1)} %get-tuple-element.13), channel_id=1, source_target_pairs={{0,16},{1,17},{2,18},{3,19},{4,20},{5,21},{6,22},{7,23},{8,24},{9,... | collective-permute-start | bytes 49160 | tf_op jit(solution)/shard_map/ppermute | solution.py:16
  3.2 3.1 %collective-permute-start.1 = (f32[2,4,512]{2,1,0:T(4,128)S(1)}, f32[2,4,512]{2,1,0:T(4,128)S(1)}, u32[]{:S(2)}, u32[]{:S(2)}) collective-permute-start(f32[2,4,512]{2,1,0:T(4,128)S(1)} %get-tuple-element.14), channel_id=1, source_target_pairs={{16,0},{17,1},{18,2},{19,3},{20,4},{21,5},{22,6},{23,7},{24,8},{25... | collective-permute-start | bytes 49160 | tf_op jit(solution)/shard_map/ppermute | solution.py:19
  6.4 5.9 %collective-permute-start.2 = (f32[2,40,4]{2,1,0:T(8,128)S(1)}, f32[2,40,4]{2,1,0:T(8,128)S(1)}, u32[]{:S(2)}, u32[]{:S(2)}) collective-permute-start(f32[2,40,4]{2,1,0:T(8,128)S(1)} %get-tuple-element.11), channel_id=1, source_target_pairs={{0,1},{1,2},{2,3},{3,4},{4,5},{5,6},{6,7},{7,8},{8,9},{9,10},{10,1... | collective-permute-start | bytes 3848 | tf_op jit(solution)/shard_map/ppermute | solution.py:16
  10.6 5.9 %collective-permute-start.3 = (f32[2,40,4]{2,1,0:T(8,128)S(1)}, f32[2,40,4]{2,1,0:T(8,128)S(1)}, u32[]{:S(2)}, u32[]{:S(2)}) collective-permute-start(f32[2,40,4]{2,1,0:T(8,128)S(1)} %get-tuple-element.12), channel_id=1, source_target_pairs={{1,0},{2,1},{3,2},{4,3},{5,4},{6,5},{7,6},{8,7},{9,8},{10,9},{11,1... | collective-permute-start | bytes 3848 | tf_op jit(solution)/shard_map/ppermute | solution.py:19
  101.3 2.6 %collective-permute-start.4 = (f32[4,512]{1,0:T(4,128)S(1)}, f32[4,512]{1,0:T(4,128)S(1)}, u32[]{:S(2)}, u32[]{:S(2)}) collective-permute-start(f32[4,512]{1,0:T(4,128)S(1)} %get-tuple-element.17), channel_id=1, source_target_pairs={{0,16},{1,17},{2,18},{3,19},{4,20},{5,21},{6,22},{7,23},{8,24},{9,... | collective-permute-start | bytes 24584 | tf_op jit(solution)/shard_map/ppermute | solution.py:16
  102.6 3.1 %collective-permute-start.5 = (f32[4,512]{1,0:T(4,128)S(1)}, f32[4,512]{1,0:T(4,128)S(1)}, u32[]{:S(2)}, u32[]{:S(2)}) collective-permute-start(f32[4,512]{1,0:T(4,128)S(1)} %get-tuple-element.18), channel_id=1, source_target_pairs={{16,0},{17,1},{18,2},{19,3},{20,4},{21,5},{22,6},{23,7},{24,8},{25... | collective-permute-start | bytes 24584 | tf_op jit(solution)/shard_map/ppermute | solution.py:19
  105.8 5.6 %collective-permute-start.6 = (f32[40,4]{1,0:T(8,128)S(1)}, f32[40,4]{1,0:T(8,128)S(1)}, u32[]{:S(2)}, u32[]{:S(2)}) collective-permute-start(f32[40,4]{1,0:T(8,128)S(1)} %get-tuple-element.15), channel_id=1, source_target_pairs={{0,1},{1,2},{2,3},{3,4},{4,5},{5,6},{6,7},{7,8},{8,9},{9,10},{10,1... | collective-permute-start | bytes 1928 | tf_op jit(solution)/shard_map/ppermute | solution.py:16
  110.0 5.7 %collective-permute-start.7 = (f32[40,4]{1,0:T(8,128)S(1)}, f32[40,4]{1,0:T(8,128)S(1)}, u32[]{:S(2)}, u32[]{:S(2)}) collective-permute-start(f32[40,4]{1,0:T(8,128)S(1)} %get-tuple-element.16), channel_id=1, source_target_pairs={{1,0},{2,1},{3,2},{4,3},{5,4},{6,5},{7,6},{8,7},{9,8},{10,9},{11,1... | collective-permute-start | bytes 1928 | tf_op jit(solution)/shard_map/ppermute | solution.py:19
where the time goes:
time: 201 us; the launch traced here: 200 us
  blocking collectives  162 us (81%)
  starting transfers between devices  17.2 us (9%)
  waiting for transfers between devices  12.4 us (6%)
  other arithmetic  4.41 us (2%)
  local copies, waits for them, and re-layouts  2.13 us (1%)
    unnamed x2, blocking collectives  82.9 us
    psum x2, blocking collectives, shards(): summed = lax.psum(whole_term, ('grp', 'tile'))  78.7 us
    ppermute x4, starting transfers between devices, extended(): lax.ppermute(lax.slice_in_dim(block, block.shape[dim] - width, None, axis...  12.1 us
    ppermute x4, waiting for transfers between devices, extended(): lax.ppermute(lax.slice_in_dim(block, 0, width, axis=dim), axis, backward)  11.9 us
    ppermute x4, starting transfers between devices, extended(): lax.ppermute(lax.slice_in_dim(block, 0, width, axis=dim), axis, backward)  5.17 us
  transfers between devices with their start and end apart: 8, of which 6 were waited for; matrix products, arithmetic and copies ran while one was open for 0% of the time, Pallas kernels for 0%

commit v1 on v0

v1 whole, which is shorter than its diff:
```python
import functools

import jax
import jax.numpy as jnp
from jax import lax
from jax.experimental import pallas as pl
from jax.experimental.pallas import tpu as pltpu
from jax.sharding import PartitionSpec as P

FAC = 16
SWEEPS = 4
OMEGA = 0.8
MIX = 0.5
LANES = 128
SUB = 8
HALO = 8

VMEM = pl.BlockSpec(memory_space=pltpu.VMEM)


def call(body, shapes, count, scratch=()):
    return pl.pallas_call(
        body,
        out_shape=[jax.ShapeDtypeStruct(s, jnp.float32) for s in shapes],
        in_specs=[VMEM] * count,
        out_specs=[VMEM] * len(shapes),
        scratch_shapes=[pltpu.VMEM(s, jnp.float32) for s in scratch],
    )


def lane_iota(shape):
    return lax.broadcasted_iota(jnp.int32, shape, len(shape) - 1)


def row_iota(shape):
    return lax.broadcasted_iota(jnp.int32, shape, 0)


def shift(x, by, axis):
    return pltpu.roll(x, by % x.shape[axis], axis)


def neighbour_sum(x):
    above, below = shift(x, 1, 0), shift(x, -1, 0)
    return above + below + shift(x + above, -1, 1) + shift(x + below, 1, 1)


def gather_lanes(x, index):
    return jnp.take_along_axis(x, index, axis=1)


def pack_lanes(strip, first):
    step = LANES // HALO
    parts = []
    for at in range(0, strip.shape[0], step):
        piece = strip[at : at + step]
        lane, row = lane_iota(piece.shape), row_iota(piece.shape)
        piece = gather_lanes(piece, first + lax.rem(lane, HALO))
        piece = jnp.where(lane // HALO == row, piece, 0.0)
        parts.append(jnp.sum(piece, axis=0, keepdims=True))
    return parts


def start_kernel(grid, rhs_ref, diag_ref, slots_ref, edge_a_ref, edge_b_ref):
    groups, tiles = grid
    g, t = lax.axis_index("grp"), lax.axis_index("tile")
    rows, cols = rhs_ref.shape
    count = groups * tiles
    per_row = cols // FAC
    even = lax.rem(g, 2) == 0
    for at, ref in ((0, rhs_ref), (HALO, diag_ref)):
        first, last = ref[:HALO, :], ref[rows - HALO :, :]
        edge_a_ref[at : at + HALO, :] = jnp.where(even, last, first)
        if groups > 2:
            edge_b_ref[at : at + HALO, :] = jnp.where(even, first, last)
    sums = []
    for ref in (rhs_ref, diag_ref):
        for a in range(rows // FAC):
            sums.append(jnp.sum(ref[a * FAC : (a + 1) * FAC, :], axis=0, keepdims=True))
    tall = jnp.concatenate(sums + [jnp.zeros((SUB - len(sums), cols), jnp.float32)], axis=0)
    pick = (
        lax.broadcasted_iota(jnp.int32, (cols, LANES), 0) // FAC
        == lax.rem(lane_iota((cols, LANES)), per_row)
    ).astype(jnp.float32)
    means = jnp.dot(
        tall, pick, precision=lax.Precision.HIGHEST, preferred_element_type=jnp.float32
    ) * (1.0 / (FAC * FAC))
    group_of = lane_iota((1, LANES)) // per_row
    coarse = jnp.zeros((1, LANES), jnp.float32)
    for k in range(LANES // per_row):
        coarse = jnp.where(group_of == k, means[k : k + 1, :], coarse)
    to_left = lax.rem(row_iota((count, LANES)), tiles) < t
    at = 0
    for ref in (rhs_ref, diag_ref):
        left = pack_lanes(ref[:, :LANES], 0)
        right = pack_lanes(ref[:, cols - LANES :], LANES - HALO)
        for one, two in zip(left, right):
            slots_ref[:, at : at + LANES] = jnp.where(
                to_left,
                jnp.broadcast_to(one, (count, LANES)),
                jnp.broadcast_to(two, (count, LANES)),
            )
            at += LANES
    slots_ref[:, at : at + LANES] = jnp.broadcast_to(coarse, (count, LANES))


def two_products(vector, factor_ref):
    high = factor_ref.shape[1] // LANES
    total = None
    for m in range(high):
        term = factor_ref[:, m * LANES : (m + 1) * LANES] * vector[m : m + 1, :]
        total = term if total is None else total + term
    inner = jnp.sum(total, axis=1, keepdims=True)
    return [
        jnp.sum(factor_ref[:, m * LANES : (m + 1) * LANES] * inner, axis=0, keepdims=True)
        for m in range(high)
    ]


def interleave(even, odd):
    return jnp.where(lane_iota(even.shape) < LANES // 2, even, odd)


def pairs(ref, at, line_ref):
    count = ref.shape[0]
    line_ref[...] = ref[:, at : at + LANES]
    return (
        line_ref[pl.ds(0, count // 2, stride=2), :],
        line_ref[pl.ds(1, count // 2, stride=2), :],
    )


def first_kernel(got_ref, factor_ref, keep_ref, send_ref, mean_ref, line_ref):
    high = factor_ref.shape[1] // LANES
    even, odd = pairs(got_ref, got_ref.shape[1] - LANES, line_ref)
    half = LANES // 2
    mean_ref[...] = interleave(shift(even, half, 1), odd)
    terms = two_products(interleave(even, shift(odd, half, 1)), factor_ref)
    own = lax.rem(lax.axis_index("grp"), 2) == 0
    for m in range(high // 2):
        low, top = terms[m], terms[m + high // 2]
        keep_ref[m : m + 1, :] = jnp.where(own, low, top)
        send_ref[m : m + 1, :] = jnp.where(own, top, low)


def inside_mask(grid, rows, cols):
    groups, tiles = grid
    g, t = lax.axis_index("grp"), lax.axis_index("tile")
    shape = (rows + 2 * HALO, cols + LANES)
    row, lane = row_iota(shape), lane_iota(shape)
    row_ok = (row < rows) | ((row < rows + HALO) & (g < groups - 1)) | ((row >= rows + HALO) & (g > 0))
    lane_ok = (
        (lane < cols)
        | ((lane < cols + HALO) & (t < tiles - 1))
        | ((lane >= cols + LANES - HALO) & (t > 0))
    )
    return row_ok & lane_ok


def unpack_lanes(lines_ref, device, at, rows):
    step = LANES // HALO
    shape = (step, LANES)
    index = row_iota(shape) * HALO + lax.rem(lane_iota(shape), HALO)
    parts = []
    for k in range(rows // step):
        line = lines_ref[at + k, pl.ds(device, 1), :]
        parts.append(gather_lanes(jnp.broadcast_to(line, shape), index))
    return jnp.concatenate(parts, axis=0)


def smooth_kernel(
    grid, got_ref, rhs_ref, diag_ref, below_ref, above_ref,
    rhs_out, diag_out, weight_out, smooth_out, coarse_out, lines_ref,
):
    groups, tiles = grid
    g, t = lax.axis_index("grp"), lax.axis_index("tile")
    rows, cols = rhs_ref.shape
    up, down = jnp.maximum(g - 1, 0), jnp.minimum(g + 1, groups - 1)
    left, right = jnp.maximum(t - 1, 0), jnp.minimum(t + 1, tiles - 1)
    inside = inside_mask(grid, rows, cols)
    for k in range(lines_ref.shape[0]):
        lines_ref[k] = got_ref[:, k * LANES : (k + 1) * LANES]
    at = 0
    for ref, out, edge in ((rhs_ref, rhs_out, 0), (diag_ref, diag_out, HALO)):
        out[:rows, :cols] = ref[...]
        out[rows : rows + HALO, :cols] = below_ref[edge : edge + HALO, :]
        out[rows + HALO :, :cols] = above_ref[edge : edge + HALO, :]
        sides = []
        for column in (right, left):
            mid = unpack_lanes(lines_ref, g * tiles + column, at, rows)
            low = unpack_lanes(lines_ref, down * tiles + column, at, rows)[:HALO]
            top = unpack_lanes(lines_ref, up * tiles + column, at, rows)[rows - HALO :]
            sides.append(jnp.concatenate([mid, low, top], axis=0))
        lane = lane_iota(sides[0].shape)
        side = jnp.where(lane < HALO, sides[0], 0.0)
        side = jnp.where(lane >= LANES - HALO, sides[1], side)
        out[:, cols:] = side
        at += rows * HALO // LANES
    rhs = jnp.where(inside, rhs_out[...], 0.0)
    diag = jnp.where(inside, diag_out[...], 0.0)
    rhs_out[...] = rhs
    diag_out[...] = diag
    weight = jnp.where(inside, OMEGA / (6.0 + diag), 0.0)
    weight_out[...] = weight
    smooth = weight * rhs
    for _ in range(SWEEPS - 1):
        smooth = (1.0 - OMEGA) * smooth + weight * (rhs + neighbour_sum(smooth))
    smooth_out[...] = smooth
    left_over = (rhs - (6.0 + diag) * smooth + neighbour_sum(smooth))[:rows, :cols]
    per_row = cols // FAC
    sums = [
        jnp.sum(left_over[a * FAC : (a + 1) * FAC], axis=0, keepdims=True)
        for a in range(rows // FAC)
    ]
    tall = jnp.concatenate(sums + [jnp.zeros((SUB - len(sums), cols), jnp.float32)], axis=0)
    pick = (
        lax.broadcasted_iota(jnp.int32, (cols, LANES), 0) // FAC
        == lax.rem(lane_iota((cols, LANES)), per_row)
    ).astype(jnp.float32)
    means = jnp.dot(
        tall, pick, precision=lax.Precision.HIGHEST, preferred_element_type=jnp.float32
    ) * (1.0 / (FAC * FAC))
    group_of = lax.rem(lane_iota((1, LANES)) // per_row, rows // FAC)
    coarse = jnp.zeros((1, LANES), jnp.float32)
    for a in range(rows // FAC):
        coarse = jnp.where(group_of == a, means[a : a + 1, :], coarse)
    coarse_out[...] = jnp.broadcast_to(coarse, (SUB, LANES))


def spread_kernel(keep_ref, came_ref, coarse_ref, slots_ref):
    count = slots_ref.shape[0]
    high = keep_ref.shape[0]
    half = keep_ref[...] + came_ref[...]
    for m in range(high):
        slots_ref[:, m * LANES : (m + 1) * LANES] = jnp.broadcast_to(
            half[m : m + 1, :], (count, LANES)
        )
    slots_ref[:, high * LANES :] = jnp.broadcast_to(coarse_ref[:1, :], (count, LANES))


def coarse_operator(value, mean, grid, blocks):
    groups, tiles = grid
    block_rows, per_row = blocks
    here = block_rows * per_row
    shape = value.shape
    lane, row = lane_iota(shape), row_iota(shape)
    device = row * (LANES // here) + lane // here
    a = lax.rem(lane, here) // per_row
    b = lax.rem(lane, per_row)
    tile, group = lax.rem(device, tiles), device // tiles
    per_line = tiles * here // LANES

    def to_right(x):
        near = shift(x, 1, 1)
        far = shift(x, here - per_row + 1, 1)
        far = jnp.where(lane < here, shift(far, 1, 0), far)
        return jnp.where(b > 0, near, jnp.where(tile > 0, far, 0.0))

    def to_left(x):
        near = shift(x, -1, 1)
        far = shift(x, -(here - per_row + 1), 1)
        far = jnp.where(lane >= LANES - here, shift(far, -1, 0), far)
        return jnp.where(b < per_row - 1, near, jnp.where(tile < tiles - 1, far, 0.0))

    def to_below(x):
        near = shift(x, per_row, 1)
        far = shift(shift(x, -(here - per_row), 1), per_line, 0)
        return jnp.where(a > 0, near, jnp.where(group > 0, far, 0.0))

    def to_above(x):
        near = shift(x, -per_row, 1)
        far = shift(shift(x, here - per_row, 1), -per_line, 0)
        return jnp.where(a < block_rows - 1, near, jnp.where(group < groups - 1, far, 0.0))

    above, below = to_below(value), to_above(value)
    sides = above + below + to_right(value) + to_left(value)
    corners = to_left(above) + to_right(below)
    edge = 2.0 * FAC - 1.0
    return mean * value + (edge * (4.0 * value - sides) + (2.0 * value - corners)) * (
        1.0 / (FAC * FAC)
    )


def second_kernel(grid, blocks, got_ref, mean_ref, factor_ref, value_ref, slots_ref, line_ref):
    groups, tiles = grid
    high = factor_ref.shape[1] // LANES
    for side in range(2):
        for m in range(high // 2):
            line = None
            for g in range(side, groups, 2):
                part = jnp.sum(
                    got_ref[g * tiles : (g + 1) * tiles, m * LANES : (m + 1) * LANES],
                    axis=0,
                    keepdims=True,
                )
                line = part if line is None else line + part
            at = side * (high // 2) + m
            value_ref[at : at + 1, :] = line
    rest = interleave(*pairs(got_ref, (high // 2) * LANES, line_ref))
    coarse = rest - MIX * coarse_operator(value_ref[...], mean_ref[...], grid, blocks)
    terms = two_products(coarse, factor_ref)
    for m, term in enumerate(terms):
        slots_ref[2 * m : 2 * m + 1, :] = term
        slots_ref[2 * m + 1 : 2 * m + 2, :] = shift(term, LANES // 2, 1)


def prolong_line(line, first, shape):
    index = jnp.broadcast_to(first + lane_iota(shape) // FAC, shape)
    return gather_lanes(jnp.broadcast_to(line, shape), index)


def last_kernel(
    grid, got_ref, value_ref, rhs_ref, diag_ref, weight_ref, smooth_ref, out_ref, field_ref
):
    groups, tiles = grid
    g, t = lax.axis_index("grp"), lax.axis_index("tile")
    rows, cols = out_ref.shape
    block_rows, per_row = rows // FAC, cols // FAC
    here = block_rows * per_row
    inside = inside_mask(grid, rows, cols)
    up, down = jnp.maximum(g - 1, 0), jnp.minimum(g + 1, groups - 1)
    left, right = jnp.maximum(t - 1, 0), jnp.minimum(t + 1, tiles - 1)

    def line_of(device):
        return value_ref[pl.ds(device * here // LANES, 1), :], lax.rem(device * here, LANES)

    bands = [(a * FAC, FAC, g, a) for a in range(block_rows)]
    bands += [(rows, HALO, down, 0), (rows + HALO, HALO, up, block_rows - 1)]
    for start, height, group, a in bands:
        shape = (SUB, LANES)
        line, at = line_of(group * tiles + t)
        parts = [
            prolong_line(line, at + a * per_row + q * (LANES // FAC), shape)
            for q in range(cols // LANES)
        ]
        line, at = line_of(group * tiles + right)
        beside = gather_lanes(
            jnp.broadcast_to(line, shape), jnp.full(shape, at + a * per_row, jnp.int32)
        )
        line, at = line_of(group * tiles + left)
        other = gather_lanes(
            jnp.broadcast_to(line, shape),
            jnp.full(shape, at + (a + 1) * per_row - 1, jnp.int32),
        )
        parts.append(jnp.where(lane_iota(shape) < LANES // 2, beside, other))
        for low in range(start, start + height, SUB):
            for q, part in enumerate(parts):
                field_ref[low : low + SUB, q * LANES : (q + 1) * LANES] = part
    field = jnp.where(inside, smooth_ref[...] + MIX * field_ref[...], 0.0)
    rhs = rhs_ref[...]
    weight = weight_ref[...]
    rest = rhs - (6.0 + diag_ref[...]) * field + neighbour_sum(field)
    smooth = weight * rest
    for _ in range(SWEEPS - 1):
        smooth = (1.0 - OMEGA) * smooth + weight * (rest + neighbour_sum(smooth))
    line = MIX * jnp.sum(got_ref[...], axis=0, keepdims=True)
    for a in range(block_rows):
        for q in range(cols // LANES):
            part = prolong_line(line, a * per_row + q * (LANES // FAC), (SUB, LANES))
            for low in range(a * FAC, (a + 1) * FAC, SUB):
                where = (slice(low, low + SUB), slice(q * LANES, (q + 1) * LANES))
                out_ref[where] = field[where] + smooth[where] + part


def shards(right_side, diagonal, inverse_factor):
    groups, tiles = lax.axis_size("grp"), lax.axis_size("tile")
    grid = (groups, tiles)
    count = groups * tiles
    rows, cols = right_side.shape
    points = inverse_factor.shape[1]
    high = points // LANES
    blocks = (rows // FAC, cols // FAC)
    everyone = ("grp", "tile")
    swap = [(i, i ^ 1) for i in range(groups)]
    g = lax.axis_index("grp")

    width = 2 * rows * HALO + LANES
    edge = (2 * HALO, cols)
    slots, edge_a, edge_b = call(
        functools.partial(start_kernel, grid), [(count, width), edge, edge], 2
    )(right_side, diagonal)
    near = lax.ppermute(edge_a, "grp", swap)
    if groups > 2:
        across = [(i, i + 1) for i in range(1, groups - 1, 2)]
        across += [(j, i) for i, j in across]
        far = lax.ppermute(edge_b, "grp", across)
        below = jnp.where(g % 2 == 0, near, far)
        above = jnp.where(g % 2 == 0, far, near)
    else:
        below, above = near, near
    got = lax.all_to_all(slots, everyone, 0, 0, tiled=True)

    half = (high // 2, LANES)
    keep, send, mean = call(first_kernel, [half, half, (high, LANES)], 2, [(count, LANES)])(
        got, inverse_factor
    )
    came = lax.ppermute(send, "grp", swap)
    wide = (rows + 2 * HALO, cols + LANES)
    rhs, diag, weight, smooth, coarse = call(
        functools.partial(smooth_kernel, grid), [wide] * 4 + [(SUB, LANES)], 5,
        [(2 * rows * HALO // LANES, count, LANES)],
    )(got, right_side, diagonal, below, above)
    (slots,) = call(spread_kernel, [(count, points // 2 + LANES)], 3)(keep, came, coarse)
    got = lax.all_to_all(slots, everyone, 0, 0, tiled=True)

    value, slots = call(
        functools.partial(second_kernel, grid, blocks), [(high, LANES), (count, LANES)], 3,
        [(count, LANES)],
    )(got, mean, inverse_factor)
    got = lax.all_to_all(slots, everyone, 0, 0, tiled=True)

    return pl.pallas_call(
        functools.partial(last_kernel, grid),
        out_shape=jax.ShapeDtypeStruct((rows, cols), jnp.float32),
        in_specs=[VMEM] * 6,
        out_specs=VMEM,
        scratch_shapes=[pltpu.VMEM(wide, jnp.float32)],
    )(got, value, rhs, diag, weight, smooth)


def solution(mesh):
    placed = (P("grp", "tile"), P("grp", "tile"), P(("grp", "tile"), None))
    return jax.shard_map(
        shards, mesh=mesh, in_specs=placed, out_specs=P("grp", "tile"), check_vma=False
    )
```

time: 201 us -> 52.5 us (0.26)
  blocking collectives: 162 us -> 20 us
  Pallas kernels: 0 us -> 11.9 us
  starting transfers between devices: 17.2 us -> 7.64 us
  waiting for transfers between devices: 12.4 us -> 7.15 us
  other arithmetic: 4.41 us -> 0 us
  local copies, waits for them, and re-layouts: 2.13 us -> 5.17 us
    unnamed x2 -> x0, blocking collectives: 82.9 us -> none
    psum x2 -> x0, blocking collectives: 78.7 us -> none  [shards(): summed = lax.psum(whole_term, ('grp', 'tile'))]
    all_to_all x0 -> x2, blocking collectives: none -> 20 us  [shards(): got = lax.all_to_all(slots, everyone, 0, 0, tiled=True)]
    ppermute x8 -> x2, starting transfers between devices: 17.2 us -> 0.32 us  [the longest x1 0.32 us: shards(): near = lax.ppermute(edge_a, 'grp', swap)]
    ppermute x8 -> x2, waiting for transfers between devices: 12.4 us -> 0.01 us  [the longest x1 0.01 us: shards(): near = lax.ppermute(edge_a, 'grp', swap)]
    pallas_call x0 -> x6, Pallas kernels: none -> 11.9 us  [the longest x1 2.38 us: shards(): call(functools.partial(smooth_kernel, grid), [wide] * 4 + [(SUB, LANES)],...]
    all_to_all x0 -> x1, starting transfers between devices: none -> 7.33 us  [shards(): got = lax.all_to_all(slots, everyone, 0, 0, tiled=True)]
    all_to_all x0 -> x1, waiting for transfers between devices: none -> 7.14 us  [shards(): got = lax.all_to_all(slots, everyone, 0, 0, tiled=True)]
  transfers between devices with their start and end apart: 8 -> 3, of which waited for: 6 -> 1; matrix products, arithmetic and copies ran while one was open for 0% -> 1% of each run, Pallas kernels for 0% -> 8%
where the time goes in v1:
time: 52.5 us; the launch traced here: 52 us
  blocking collectives  20 us (38%)
  Pallas kernels  11.9 us (23%)
  starting transfers between devices  7.64 us (15%)
  waiting for transfers between devices  7.15 us (14%)
  local copies, waits for them, and re-layouts  5.17 us (10%)
    all_to_all x2, blocking collectives, shards(): got = lax.all_to_all(slots, everyone, 0, 0, tiled=True)  20 us
    all_to_all x1, starting transfers between devices, shards(): got = lax.all_to_all(slots, everyone, 0, 0, tiled=True)  7.33 us
    all_to_all x1, waiting for transfers between devices, shards(): got = lax.all_to_all(slots, everyone, 0, 0, tiled=True)  7.14 us
    all_to_all x2, local copies, waits for them, and re-layouts, shards(): got = lax.all_to_all(slots, everyone, 0, 0, tiled=True)  2.66 us
    unnamed x8, local copies, waits for them, and re-layouts  2.51 us
    pallas_call x1, Pallas kernels, shards(): call(functools.partial(smooth_kernel, grid), [wide] * 4 + [(SUB, LANES)],...  2.38 us
    pallas_call x1, Pallas kernels, shards(): pl.pallas_call(functools.partial(last_kernel, grid), out_shape=jax.ShapeD...  2.35 us
    pallas_call x1, Pallas kernels, shards(): call(functools.partial(second_kernel, grid, blocks), [(high, LANES), (cou...  2.14 us
  transfers between devices with their start and end apart: 3, of which 1 were waited for; matrix products, arithmetic and copies ran while one was open for 1% of the time, Pallas kernels for 8%

profile of v1, /device:TPU:0, one launch (start us, length us, event | category | flops | bytes accessed | tf_op | source)
XLA Modules:
  0.0 52.0 jit_solution(9442359766600593241)
XLA Ops:
  0.0 1.8 %shard_map.37 = (f32[32,640]{1,0:T(8,128)}, f32[16,512]{1,0:T(8,128)}, f32[16,512]{1,0:T(8,128)}) custom-call(f32[32,512]{1,0:T(8,128)} %rhs_ref.3, f32[32,512]{1,0:T(8,128)} %diag_ref.3), custom_call_target="tpu_custom_call" | custom-call | tf_op jit(solution)/shard_map/pallas_call | solution.py:379
  1.8 1.6 %copy.4 = f32[32,1,640]{2,1,0:T(1,128)} copy(f32[32,1,640]{2,0,1:T(8,128)} %bitcast.16) | data formatting | bytes 163840 | tf_op jit(solution)/shard_map/all_to_all | solution.py:391
  3.4 0.0 copy-start.2
  3.4 7.3 %all-to-all-start = ((f32[32,1,640]{2,1,0:T(1,128)}), f32[32,1,640]{2,1,0:T(1,128)S(1)}, u32[]{:S(2)}, u32[]{:S(2)}) async-start(f32[32,1,640]{2,1,0:T(1,128)} %copy.4), calls=%async_computation | async-start | bytes 163840 | tf_op jit(solution)/shard_map/all_to_all | solution.py:391
  10.7 0.0 copy-done.2
  10.7 0.3 collective-permute-start.1
  11.0 7.1 %all-to-all-done = f32[32,1,640]{2,1,0:T(1,128)S(1)} async-done(((f32[32,1,640]{2,1,0:T(1,128)}), f32[32,1,640]{2,1,0:T(1,128)S(1)}, u32[]{:S(2)}, u32[]{:S(2)}) %all-to-all-start) | async-done | bytes 81952 | tf_op jit(solution)/shard_map/all_to_all | solution.py:391
  18.2 0.6 %copy.12 = f32[32,1,640]{2,0,1:T(8,128)} copy(f32[32,1,640]{2,1,0:T(1,128)S(1)} %all-to-all-done) | data formatting | bytes 163840
  18.8 1.9 %shard_map.38 = (f32[8,128]{1,0:T(8,128)}, f32[8,128]{1,0:T(8,128)}, f32[16,128]{1,0:T(8,128)}) custom-call(f32[32,640]{1,0:T(8,128)} %bitcast.12, f32[64,2048]{1,0:T(8,128)} %factor_ref.3), custom_call_target="tpu_custom_call" | custom-call | tf_op jit(solution)/shard_map/pallas_call | solution.py:394
  20.7 0.0 collective-permute-start
  20.7 0.0 collective-permute-done.1.below_ref.above_ref
  20.7 0.0 copy-start
  20.8 0.6 %copy-done = f32[16,512]{1,0:T(8,128)} copy-done((f32[16,512]{1,0:T(8,128)}, f32[16,512]{1,0:T(8,128)S(1)}, u32[]{:S(2)}) %copy-start) | copy-done | bytes 32792
  21.4 2.4 %shard_map.39 = (f32[48,640]{1,0:T(8,128)}, f32[48,640]{1,0:T(8,128)}, f32[48,640]{1,0:T(8,128)}, f32[48,640]{1,0:T(8,128)}, f32[8,128]{1,0:T(8,128)}) custom-call(f32[32,640]{1,0:T(8,128)} %bitcast.13, f32[32,512]{1,0:T(8,128)} %rhs_ref.3, f32[32,512]{1,0:T(8,128)} %diag_ref.3, f32[16,512]{1,0:T(8,128)} %copy-done, f32[16,512]{1,0:T(8,128)} %copy-done), custom_call_target="tpu_custom_call" | custom-call | tf_op jit(solution)/shard_map/pallas_call | solution.py:399
  23.7 0.0 collective-permute-done.came_ref
  23.7 0.0 copy-start.1
  23.7 0.6 %copy-done.1 = f32[8,128]{1,0:T(8,128)} copy-done((f32[8,128]{1,0:T(8,128)}, f32[8,128]{1,0:T(8,128)S(1)}, u32[]{:S(2)}) %copy-start.1) | copy-done | bytes 4120
  24.3 1.4 %shard_map.40 = f32[32,1152]{1,0:T(8,128)} custom-call(f32[8,128]{1,0:T(8,128)} %get-tuple-element.18.keep_ref, f32[8,128]{1,0:T(8,128)} %copy-done.1, f32[8,128]{1,0:T(8,128)} %get-tuple-element.21.coarse_ref), custom_call_target="tpu_custom_call" | custom-call | tf_op jit(solution)/shard_map/pallas_call | solution.py:403
  25.7 1.1 %copy.5 = f32[32,1,1152]{2,1,0:T(1,128)S(1)} copy(f32[32,1,1152]{2,0,1:T(8,128)} %bitcast.14) | data formatting | bytes 294912 | tf_op jit(solution)/shard_map/all_to_all | solution.py:404
  26.8 9.9 %all_to_all.33 = f32[32,1,1152]{2,1,0:T(1,128)S(1)} all-to-all(f32[32,1,1152]{2,1,0:T(1,128)S(1)} %copy.5), channel_id=1, replica_groups=mesh['grp'=2,'tile'=16] {'grp','tile'}, dimensions={0} | all-to-all | bytes 294912 | tf_op jit(solution)/shard_map/all_to_all | solution.py:404
  36.7 0.7 %copy.11 = f32[32,1,1152]{2,0,1:T(8,128)} copy(f32[32,1,1152]{2,1,0:T(1,128)S(1)} %all_to_all.33) | data formatting | bytes 294912
  37.4 2.1 %shard_map.41 = (f32[16,128]{1,0:T(8,128)}, f32[32,128]{1,0:T(8,128)}) custom-call(f32[32,1152]{1,0:T(8,128)} %bitcast.15, f32[16,128]{1,0:T(8,128)} %get-tuple-element.22.mean_ref, f32[64,2048]{1,0:T(8,128)} %factor_ref.3), custom_call_target="tpu_custom_call" | custom-call | tf_op jit(solution)/shard_map/pallas_call | solution.py:406
  39.5 10.1 %all_to_all.34 = f32[32,1,128]{2,1,0:T(1,128)} all-to-all(f32[32,1,128]{2,1,0:T(1,128)} %bitcast.18), channel_id=1, replica_groups=mesh['grp'=2,'tile'=16] {'grp','tile'}, dimensions={0} | all-to-all | bytes 32768 | tf_op jit(solution)/shard_map/all_to_all | solution.py:410
  49.6 2.4 %shard_map.42 = f32[32,512]{1,0:T(8,128)} custom-call(f32[32,128]{1,0:T(8,128)} %bitcast.17, f32[16,128]{1,0:T(8,128)} %get-tuple-element.24.value_ref, f32[48,640]{1,0:T(8,128)} %get-tuple-element.25.rhs_ref, f32[48,640]{1,0:T(8,128)} %get-tuple-element.26.diag_ref, f32[48,640]{1,0:T(8,128)} %get-tuple-element.27.weight_ref, ...), custom_call_target="tpu_custom_call" | custom-call | tf_op jit(solution)/shard_map/pallas_call | solution.py:412
Async XLA Ops:
  3.4 7.3 %copy-start.2 = (f32[16,512]{1,0:T(8,128)S(1)}, f32[16,512]{1,0:T(8,128)}, u32[]{:S(2)}) copy-start(f32[16,512]{1,0:T(8,128)} %get-tuple-element.20) | copy-start | bytes 98308
  3.4 14.8 %all-to-all-start = ((f32[32,1,640]{2,1,0:T(1,128)}), f32[32,1,640]{2,1,0:T(1,128)S(1)}, u32[]{:S(2)}, u32[]{:S(2)}) async-start(f32[32,1,640]{2,1,0:T(1,128)} %copy.4), calls=%async_computation | async-start | bytes 163840 | tf_op jit(solution)/shard_map/all_to_all | solution.py:391
  10.7 10.0 %collective-permute-start.1 = (f32[16,512]{1,0:T(8,128)S(1)}, f32[16,512]{1,0:T(8,128)S(1)}, u32[]{:S(2)}, u32[]{:S(2)}) collective-permute-start(f32[16,512]{1,0:T(8,128)S(1)} %copy-done.2), channel_id=1, source_target_pairs={{0,16},{16,0},{1,17},{17,1},{2,18},{18,2},{3,19},{19,3},{4,20},{20... | collective-permute-start | bytes 98312 | tf_op jit(solution)/shard_map/ppermute | solution.py:382
  20.7 3.0 %collective-permute-start = (f32[8,128]{1,0:T(8,128)}, f32[8,128]{1,0:T(8,128)S(1)}, u32[]{:S(2)}, u32[]{:S(2)}) collective-permute-start(f32[8,128]{1,0:T(8,128)} %get-tuple-element.19), channel_id=1, source_target_pairs={{0,16},{16,0},{1,17},{17,1},{2,18},{18,2},{3,19},{19,3},{4,20},{20... | collective-permute-start | bytes 12296 | tf_op jit(solution)/shard_map/ppermute | solution.py:397
  20.7 0.6 %copy-start = (f32[16,512]{1,0:T(8,128)}, f32[16,512]{1,0:T(8,128)S(1)}, u32[]{:S(2)}) copy-start(f32[16,512]{1,0:T(8,128)S(1)} %collective-permute-done.1.below_ref.above_ref) | copy-start | bytes 98308
  23.7 0.6 %copy-start.1 = (f32[8,128]{1,0:T(8,128)}, f32[8,128]{1,0:T(8,128)S(1)}, u32[]{:S(2)}) copy-start(f32[8,128]{1,0:T(8,128)S(1)} %collective-permute-done.came_ref) | copy-start | bytes 12292

commit v2 on v1

--- a/solution.py
+++ b/solution.py
@@ -18,6 +18,9 @@
 VMEM = pl.BlockSpec(memory_space=pltpu.VMEM)
 
 
+LIMIT = 8 * 1024 * 1024
+
+
 def call(body, shapes, count, scratch=()):
     return pl.pallas_call(
         body,
@@ -25,6 +28,7 @@
         in_specs=[VMEM] * count,
         out_specs=[VMEM] * len(shapes),
         scratch_shapes=[pltpu.VMEM(s, jnp.float32) for s in scratch],
+        compiler_params=pltpu.CompilerParams(vmem_limit_bytes=LIMIT),
     )
 
 
@@ -90,18 +94,14 @@
     for k in range(LANES // per_row):
         coarse = jnp.where(group_of == k, means[k : k + 1, :], coarse)
     to_left = lax.rem(row_iota((count, LANES)), tiles) < t
-    at = 0
+    lines = []
     for ref in (rhs_ref, diag_ref):
         left = pack_lanes(ref[:, :LANES], 0)
         right = pack_lanes(ref[:, cols - LANES :], LANES - HALO)
-        for one, two in zip(left, right):
-            slots_ref[:, at : at + LANES] = jnp.where(
-                to_left,
-                jnp.broadcast_to(one, (count, LANES)),
-                jnp.broadcast_to(two, (count, LANES)),
-            )
-            at += LANES
-    slots_ref[:, at : at + LANES] = jnp.broadcast_to(coarse, (count, LANES))
+        lines += [jnp.where(to_left, one, two) for one, two in zip(left, right)]
+    lines.append(jnp.broadcast_to(coarse, (count, LANES)))
+    for k, line in enumerate(lines):
+        slots_ref[pl.ds(k, count, stride=len(lines)), :] = line
 
 
 def two_products(vector, factor_ref):
@@ -121,18 +121,16 @@
     return jnp.where(lane_iota(even.shape) < LANES // 2, even, odd)
 
 
-def pairs(ref, at, line_ref):
-    count = ref.shape[0]
-    line_ref[...] = ref[:, at : at + LANES]
-    return (
-        line_ref[pl.ds(0, count // 2, stride=2), :],
-        line_ref[pl.ds(1, count // 2, stride=2), :],
-    )
-
-
-def first_kernel(got_ref, factor_ref, keep_ref, send_ref, mean_ref, line_ref):
+def pairs(ref, line, width):
+    count = ref.shape[0] // width
+    return [
+        ref[pl.ds(line + side * width, count // 2, stride=2 * width), :] for side in range(2)
+    ]
+
+
+def first_kernel(width, got_ref, factor_ref, keep_ref, send_ref, mean_ref):
     high = factor_ref.shape[1] // LANES
-    even, odd = pairs(got_ref, got_ref.shape[1] - LANES, line_ref)
+    even, odd = pairs(got_ref, width - 1, width)
     half = LANES // 2
     mean_ref[...] = interleave(shift(even, half, 1), odd)
     terms = two_products(interleave(even, shift(odd, half, 1)), factor_ref)
@@ -157,20 +155,20 @@
     return row_ok & lane_ok
 
 
-def unpack_lanes(lines_ref, device, at, rows):
+def unpack_lanes(got_ref, line, rows):
     step = LANES // HALO
     shape = (step, LANES)
     index = row_iota(shape) * HALO + lax.rem(lane_iota(shape), HALO)
     parts = []
     for k in range(rows // step):
-        line = lines_ref[at + k, pl.ds(device, 1), :]
-        parts.append(gather_lanes(jnp.broadcast_to(line, shape), index))
+        piece = jnp.broadcast_to(got_ref[pl.ds(line + k, 1), :], shape)
+        parts.append(gather_lanes(piece, index))
     return jnp.concatenate(parts, axis=0)
 
 
 def smooth_kernel(
-    grid, got_ref, rhs_ref, diag_ref, below_ref, above_ref,
-    rhs_out, diag_out, weight_out, smooth_out, coarse_out, lines_ref,
+    grid, width, got_ref, rhs_ref, diag_ref, below_ref, above_ref,
+    rhs_out, diag_out, weight_out, smooth_out, coarse_out,
 ):
     groups, tiles = grid
     g, t = lax.axis_index("grp"), lax.axis_index("tile")
@@ -178,8 +176,6 @@
     up, down = jnp.maximum(g - 1, 0), jnp.minimum(g + 1, groups - 1)
     left, right = jnp.maximum(t - 1, 0), jnp.minimum(t + 1, tiles - 1)
     inside = inside_mask(grid, rows, cols)
-    for k in range(lines_ref.shape[0]):
-        lines_ref[k] = got_ref[:, k * LANES : (k + 1) * LANES]
     at = 0
     for ref, out, edge in ((rhs_ref, rhs_out, 0), (diag_ref, diag_out, HALO)):
         out[:rows, :cols] = ref[...]
@@ -187,9 +183,9 @@
         out[rows + HALO :, :cols] = above_ref[edge : edge + HALO, :]
         sides = []
         for column in (right, left):
-            mid = unpack_lanes(lines_ref, g * tiles + column, at, rows)
-            low = unpack_lanes(lines_ref, down * tiles + column, at, rows)[:HALO]
-            top = unpack_lanes(lines_ref, up * tiles + column, at, rows)[rows - HALO :]
+            mid = unpack_lanes(got_ref, (g * tiles + column) * width + at, rows)
+            low = unpack_lanes(got_ref, (down * tiles + column) * width + at, rows)[:HALO]
+            top = unpack_lanes(got_ref, (up * tiles + column) * width + at, rows)[rows - HALO :]
             sides.append(jnp.concatenate([mid, low, top], axis=0))
         lane = lane_iota(sides[0].shape)
         side = jnp.where(lane < HALO, sides[0], 0.0)
@@ -228,14 +224,12 @@
 
 
 def spread_kernel(keep_ref, came_ref, coarse_ref, slots_ref):
-    count = slots_ref.shape[0]
     high = keep_ref.shape[0]
+    width = high + 1
     half = keep_ref[...] + came_ref[...]
-    for m in range(high):
-        slots_ref[:, m * LANES : (m + 1) * LANES] = jnp.broadcast_to(
-            half[m : m + 1, :], (count, LANES)
-        )
-    slots_ref[:, high * LANES :] = jnp.broadcast_to(coarse_ref[:1, :], (count, LANES))
+    for device in range(slots_ref.shape[0] // width):
+        slots_ref[device * width : device * width + high, :] = half
+        slots_ref[device * width + high : (device + 1) * width, :] = coarse_ref[:1, :]
 
 
 def coarse_operator(value, mean, grid, blocks):
@@ -281,22 +275,18 @@
     )
 
 
-def second_kernel(grid, blocks, got_ref, mean_ref, factor_ref, value_ref, slots_ref, line_ref):
-    groups, tiles = grid
-    high = factor_ref.shape[1] // LANES
+def second_kernel(grid, blocks, got_ref, mean_ref, factor_ref, value_ref, slots_ref):
+    groups, tiles = grid
+    high = factor_ref.shape[1] // LANES // 2
+    width = high + 1
     for side in range(2):
-        for m in range(high // 2):
-            line = None
-            for g in range(side, groups, 2):
-                part = jnp.sum(
-                    got_ref[g * tiles : (g + 1) * tiles, m * LANES : (m + 1) * LANES],
-                    axis=0,
-                    keepdims=True,
-                )
-                line = part if line is None else line + part
-            at = side * (high // 2) + m
-            value_ref[at : at + 1, :] = line
-    rest = interleave(*pairs(got_ref, (high // 2) * LANES, line_ref))
+        total = None
+        for g in range(side, groups, 2):
+            for device in range(g * tiles, (g + 1) * tiles):
+                part = got_ref[device * width : device * width + high, :]
+                total = part if total is None else total + part
+        value_ref[side * high : (side + 1) * high, :] = total
+    rest = interleave(*pairs(got_ref, high, width))
     coarse = rest - MIX * coarse_operator(value_ref[...], mean_ref[...], grid, blocks)
     terms = two_products(coarse, factor_ref)
     for m, term in enumerate(terms):
@@ -309,12 +299,12 @@
     return gather_lanes(jnp.broadcast_to(line, shape), index)
 
 
-def last_kernel(
-    grid, got_ref, value_ref, rhs_ref, diag_ref, weight_ref, smooth_ref, out_ref, field_ref
+def resmooth_kernel(
+    grid, value_ref, rhs_ref, diag_ref, weight_ref, smooth_ref, base_ref, field_ref
 ):
     groups, tiles = grid
     g, t = lax.axis_index("grp"), lax.axis_index("tile")
-    rows, cols = out_ref.shape
+    rows, cols = base_ref.shape
     block_rows, per_row = rows // FAC, cols // FAC
     here = block_rows * per_row
     inside = inside_mask(grid, rows, cols)
@@ -353,13 +343,19 @@
     smooth = weight * rest
     for _ in range(SWEEPS - 1):
         smooth = (1.0 - OMEGA) * smooth + weight * (rest + neighbour_sum(smooth))
+    base_ref[...] = field[:rows, :cols] + smooth[:rows, :cols]
+
+
+def last_kernel(got_ref, base_ref, out_ref):
+    rows, cols = out_ref.shape
+    per_row = cols // FAC
     line = MIX * jnp.sum(got_ref[...], axis=0, keepdims=True)
-    for a in range(block_rows):
+    for a in range(rows // FAC):
         for q in range(cols // LANES):
             part = prolong_line(line, a * per_row + q * (LANES // FAC), (SUB, LANES))
             for low in range(a * FAC, (a + 1) * FAC, SUB):
                 where = (slice(low, low + SUB), slice(q * LANES, (q + 1) * LANES))
-                out_ref[where] = field[where] + smooth[where] + part
+                out_ref[where] = base_ref[where] + part
 
 
 def shards(right_side, diagonal, inverse_factor):
@@ -374,10 +370,15 @@
     swap = [(i, i ^ 1) for i in range(groups)]
     g = lax.axis_index("grp")
 
-    width = 2 * rows * HALO + LANES
+    def exchange(slots):
+        lines = slots.shape[0] // count
+        got = lax.all_to_all(slots.reshape(count, lines * LANES), everyone, 0, 0, tiled=True)
+        return got.reshape(count * lines, LANES)
+
+    width = 2 * rows * HALO // LANES + 1
     edge = (2 * HALO, cols)
     slots, edge_a, edge_b = call(
-        functools.partial(start_kernel, grid), [(count, width), edge, edge], 2
+        functools.partial(start_kernel, grid), [(count * width, LANES), edge, edge], 2
     )(right_side, diagonal)
     near = lax.ppermute(edge_a, "grp", swap)
     if groups > 2:
@@ -388,34 +389,29 @@
         above = jnp.where(g % 2 == 0, far, near)
     else:
         below, above = near, near
-    got = lax.all_to_all(slots, everyone, 0, 0, tiled=True)
+    got = exchange(slots)
 
     half = (high // 2, LANES)
-    keep, send, mean = call(first_kernel, [half, half, (high, LANES)], 2, [(count, LANES)])(
-        got, inverse_factor
-    )
+    keep, send, mean = call(
+        functools.partial(first_kernel, width), [half, half, (high, LANES)], 2
+    )(got, inverse_factor)
     came = lax.ppermute(send, "grp", swap)
     wide = (rows + 2 * HALO, cols + LANES)
     rhs, diag, weight, smooth, coarse = call(
-        functools.partial(smooth_kernel, grid), [wide] * 4 + [(SUB, LANES)], 5,
-        [(2 * rows * HALO // LANES, count, LANES)],
+        functools.partial(smooth_kernel, grid, width), [wide] * 4 + [(SUB, LANES)], 5
     )(got, right_side, diagonal, below, above)
-    (slots,) = call(spread_kernel, [(count, points // 2 + LANES)], 3)(keep, came, coarse)
-    got = lax.all_to_all(slots, everyone, 0, 0, tiled=True)
+    (slots,) = call(spread_kernel, [(count * (high // 2 + 1), LANES)], 3)(keep, came, coarse)
+    got = exchange(slots)
 
     value, slots = call(
-        functools.partial(second_kernel, grid, blocks), [(high, LANES), (count, LANES)], 3,
-        [(count, LANES)],
+        functools.partial(second_kernel, grid, blocks), [(high, LANES), (count, LANES)], 3
     )(got, mean, inverse_factor)
-    got = lax.all_to_all(slots, everyone, 0, 0, tiled=True)
-
-    return pl.pallas_call(
-        functools.partial(last_kernel, grid),
-        out_shape=jax.ShapeDtypeStruct((rows, cols), jnp.float32),
-        in_specs=[VMEM] * 6,
-        out_specs=VMEM,
-        scratch_shapes=[pltpu.VMEM(wide, jnp.float32)],
-    )(got, value, rhs, diag, weight, smooth)
+    got = exchange(slots)
+    (base,) = call(
+        functools.partial(resmooth_kernel, grid), [(rows, cols)], 5, [wide]
+    )(value, rhs, diag, weight, smooth)
+    (field,) = call(last_kernel, [(rows, cols)], 2)(got, base)
+    return field
 
 
 def solution(mesh):

time: 52.5 us -> 41.8 us (0.80)
  blocking collectives: 20 us -> 9.93 us
  Pallas kernels: 11.9 us -> 4.29 us
  waiting for transfers between devices: 7.15 us -> 13.6 us
  starting transfers between devices: 7.64 us -> 10.3 us
  local copies, waits for them, and re-layouts: 5.17 us -> 3.25 us
    all_to_all x2 -> x1, blocking collectives: 20 us -> 9.93 us  [exchange(): lax.all_to_all(slots.reshape(count, lines * LANES), everyone, 0, 0, tiled...]
    pallas_call x5 -> x6, Pallas kernels: 9.81 us -> 3.3 us  [the longest x1 0.9 us: shards(): call(functools.partial(start_kernel, grid), [(count * width, LANES), edge...]
    all_to_all x1 -> x2, waiting for transfers between devices: 7.14 us -> 13.6 us  [exchange(): lax.all_to_all(slots.reshape(count, lines * LANES), everyone, 0, 0, tiled...]
    all_to_all x2 -> x0, local copies, waits for them, and re-layouts: 2.66 us -> none  [shards(): got = lax.all_to_all(slots, everyone, 0, 0, tiled=True)]
    all_to_all x1 -> x2, starting transfers between devices: 7.33 us -> 9.87 us  [exchange(): lax.all_to_all(slots.reshape(count, lines * LANES), everyone, 0, 0, tiled...]
    pallas_call x1, Pallas kernels: 2.14 us -> 0.99 us  [shards(): call(functools.partial(second_kernel, grid, blocks), [(high, LANES), (cou...]
    unnamed x8 -> x12, local copies, waits for them, and re-layouts: 2.51 us -> 3.25 us
  transfers between devices with their start and end apart: 3 -> 4, of which waited for: 1 -> 2; matrix products, arithmetic and copies ran while one was open for 1% -> 0% of each run, Pallas kernels for 8% -> 4%
where the time goes in v2:
time: 41.8 us; the launch traced here: 41.4 us
  waiting for transfers between devices  13.6 us (33%)
  starting transfers between devices  10.3 us (25%)
  blocking collectives  9.93 us (24%)
  Pallas kernels  4.29 us (10%)
  local copies, waits for them, and re-layouts  3.25 us (8%)
    all_to_all x2, waiting for transfers between devices, exchange(): lax.all_to_all(slots.reshape(count, lines * LANES), everyone, 0, 0, tiled...  13.6 us
    all_to_all x1, blocking collectives, exchange(): lax.all_to_all(slots.reshape(count, lines * LANES), everyone, 0, 0, tiled...  9.93 us
    all_to_all x2, starting transfers between devices, exchange(): lax.all_to_all(slots.reshape(count, lines * LANES), everyone, 0, 0, tiled...  9.87 us
    unnamed x12, local copies, waits for them, and re-layouts  3.25 us
    pallas_call x1, Pallas kernels, shards(): call(functools.partial(second_kernel, grid, blocks), [(high, LANES), (cou...  0.99 us
    pallas_call x1, Pallas kernels, shards(): call(functools.partial(start_kernel, grid), [(count * width, LANES), edge...  0.9 us
  transfers between devices with their start and end apart: 4, of which 2 were waited for; matrix products, arithmetic and copies ran while one was open for 0% of the time, Pallas kernels for 4%

profile of v2, /device:TPU:0, one launch (start us, length us, event | category | flops | bytes accessed | tf_op | source)
XLA Modules:
  0.0 41.4 jit_solution(7668810170135222557)
XLA Ops:
  0.0 0.0 copy-start.2
  0.0 0.8 %copy-done.2 = f32[32,512]{1,0:T(8,128)S(1)} copy-done((f32[32,512]{1,0:T(8,128)S(1)}, f32[32,512]{1,0:T(8,128)}, u32[]{:S(2)}) %copy-start.2) | copy-done | bytes 65560
  0.8 0.0 copy-start.4
  0.8 0.8 %copy-done.4 = f32[32,512]{1,0:T(8,128)S(1)} copy-done((f32[32,512]{1,0:T(8,128)S(1)}, f32[32,512]{1,0:T(8,128)}, u32[]{:S(2)}) %copy-start.4) | copy-done | bytes 65560
  1.7 0.9 %shard_map.37 = (f32[160,128]{1,0:T(8,128)}, f32[16,512]{1,0:T(8,128)S(1)}, f32[16,512]{1,0:T(8,128)}) custom-call(f32[32,512]{1,0:T(8,128)S(1)} %copy-done.2, f32[32,512]{1,0:T(8,128)S(1)} %copy-done.4), custom_call_target="tpu_custom_call" | custom-call | tf_op jit(solution)/shard_map/pallas_call | solution.py:380
  2.6 0.0 copy-start.5
  2.6 7.3 %all-to-all-start = ((f32[32,1,640]{2,1,0:T(1,128)}), f32[32,1,640]{2,1,0:T(1,128)S(1)}, u32[]{:S(2)}, u32[]{:S(2)}) async-start(f32[32,1,640]{2,1,0:T(1,128)} %bitcast), calls=%async_computation | async-start | bytes 163840 | tf_op jit(solution)/shard_map/all_to_all | solution.py:375
  9.9 0.3 collective-permute-start.1
  10.2 7.2 %all-to-all-done = f32[32,1,640]{2,1,0:T(1,128)S(1)} async-done(((f32[32,1,640]{2,1,0:T(1,128)}), f32[32,1,640]{2,1,0:T(1,128)S(1)}, u32[]{:S(2)}, u32[]{:S(2)}) %all-to-all-start) | async-done | bytes 81952 | tf_op jit(solution)/shard_map/all_to_all | solution.py:375
  17.4 0.0 copy-start
  17.4 1.0 %copy-done = f32[64,2048]{1,0:T(8,128)S(1)} copy-done((f32[64,2048]{1,0:T(8,128)S(1)}, f32[64,2048]{1,0:T(8,128)}, u32[]{:S(2)}) %copy-start) | copy-done | bytes 524312
  18.4 0.0 copy-start.3
  18.4 0.0 copy-start.1
  18.4 0.2 shard_map.38
  18.7 0.1 collective-permute-start
  18.7 0.0 collective-permute-done.1.below_ref.above_ref
  18.7 0.0 copy-done.5
  18.8 0.5 %copy-done.3 = f32[32,512]{1,0:T(8,128)S(1)} copy-done((f32[32,512]{1,0:T(8,128)S(1)}, f32[32,512]{1,0:T(8,128)}, u32[]{:S(2)}) %copy-start.3) | copy-done | bytes 65560
  19.3 0.8 %shard_map.39 = (f32[48,640]{1,0:T(8,128)S(1)}, f32[48,640]{1,0:T(8,128)S(1)}, f32[48,640]{1,0:T(8,128)S(1)}, f32[48,640]{1,0:T(8,128)S(1)}, f32[8,128]{1,0:T(8,128)S(1)}) custom-call(f32[160,128]{1,0:T(8,128)S(1)} %bitcast.9, f32[32,512]{1,0:T(8,128)S(1)} %copy-done.3, f32[32,512]{1,0:T(8,128)S(1)} %copy-done.5, ...), custom_call_target="tpu_custom_call" | custom-call | tf_op jit(solution)/shard_map/pallas_call | solution.py:400
  20.1 0.0 collective-permute-done.came_ref
  20.1 9.9 %all_to_all.29 = f32[32,1,1152]{2,1,0:T(1,128)S(1)} all-to-all(f32[32,1,1152]{2,1,0:T(1,128)S(1)} %bitcast.10), channel_id=1, replica_groups=mesh['grp'=2,'tile'=16] {'grp','tile'}, dimensions={0} | all-to-all | bytes 294912 | tf_op jit(solution)/shard_map/all_to_all | solution.py:375
  30.1 0.0 copy-done.1
  30.1 1.0 %shard_map.41 = (f32[16,128]{1,0:T(8,128)S(1)}, f32[32,128]{1,0:T(8,128)}) custom-call(f32[288,128]{1,0:T(8,128)S(1)} %bitcast.11, f32[16,128]{1,0:T(8,128)S(1)} %get-tuple-element.22.mean_ref, f32[64,2048]{1,0:T(8,128)S(1)} %copy-done.1), custom_call_target="tpu_custom_call" | custom-call | tf_op jit(solution)/shard_map/pallas_call | solution.py:406
  31.1 2.5 %all-to-all-start.2 = ((f32[32,1,128]{2,1,0:T(1,128)}), f32[32,1,128]{2,1,0:T(1,128)S(1)}, u32[]{:S(2)}, u32[]{:S(2)}) async-start(f32[32,1,128]{2,1,0:T(1,128)} %bitcast.5), calls=%async_computation.2 | async-start | bytes 32768 | tf_op jit(solution)/shard_map/all_to_all | solution.py:375
  33.6 0.6 %shard_map.42.base_ref = f32[32,512]{1,0:T(8,128)S(1)} custom-call(f32[16,128]{1,0:T(8,128)S(1)} %get-tuple-element.24.value_ref, f32[48,640]{1,0:T(8,128)S(1)} %get-tuple-element.25.rhs_ref, f32[48,640]{1,0:T(8,128)S(1)} %get-tuple-element.26.diag_ref, f32[48,640]{1,0:T(8,128)S(1)} %get-tuple-element.27.weight_ref, f32[48,640]{1,0:T(8,128)S(1)} %get-tuple-element.28.smooth_ref), custom_call_target="tpu_custom_call" | custom-call | tf_op jit(solution)/shard_map/pallas_call | solution.py:410
  34.2 6.5 %all-to-all-done.2 = f32[32,1,128]{2,1,0:T(1,128)S(1)} async-done(((f32[32,1,128]{2,1,0:T(1,128)}), f32[32,1,128]{2,1,0:T(1,128)S(1)}, u32[]{:S(2)}, u32[]{:S(2)}) %all-to-all-start.2) | async-done | bytes 16416 | tf_op jit(solution)/shard_map/all_to_all | solution.py:375
  40.7 0.7 %shard_map.43 = f32[32,512]{1,0:T(8,128)} custom-call(f32[32,128]{1,0:T(8,128)S(1)} %bitcast.12, f32[32,512]{1,0:T(8,128)S(1)} %shard_map.42.base_ref), custom_call_target="tpu_custom_call" | custom-call | tf_op jit(solution)/shard_map/pallas_call | solution.py:413
  (1 shorter events, 0.0 us)
Async XLA Ops:
  0.0 0.8 %copy-start.2 = (f32[32,512]{1,0:T(8,128)S(1)}, f32[32,512]{1,0:T(8,128)}, u32[]{:S(2)}) copy-start(f32[32,512]{1,0:T(8,128)} %rhs_ref.3) | copy-start | bytes 196612
  0.8 0.8 %copy-start.4 = (f32[32,512]{1,0:T(8,128)S(1)}, f32[32,512]{1,0:T(8,128)}, u32[]{:S(2)}) copy-start(f32[32,512]{1,0:T(8,128)} %diag_ref.3) | copy-start | bytes 196612
  2.6 16.2 %copy-start.5 = (f32[32,512]{1,0:T(8,128)S(1)}, f32[32,512]{1,0:T(8,128)}, u32[]{:S(2)}) copy-start(f32[32,512]{1,0:T(8,128)} %diag_ref.3) | copy-start | bytes 196612
  2.6 14.8 %all-to-all-start = ((f32[32,1,640]{2,1,0:T(1,128)}), f32[32,1,640]{2,1,0:T(1,128)S(1)}, u32[]{:S(2)}, u32[]{:S(2)}) async-start(f32[32,1,640]{2,1,0:T(1,128)} %bitcast), calls=%async_computation | async-start | bytes 163840 | tf_op jit(solution)/shard_map/all_to_all | solution.py:375
  9.9 8.8 %collective-permute-start.1 = (f32[16,512]{1,0:T(8,128)S(1)}, f32[16,512]{1,0:T(8,128)S(1)}, u32[]{:S(2)}, u32[]{:S(2)}) collective-permute-start(f32[16,512]{1,0:T(8,128)S(1)} %get-tuple-element.20), channel_id=1, source_target_pairs={{0,16},{16,0},{1,17},{17,1},{2,18},{18,2},{3,19},{19,3},{4,20},{20... | collective-permute-start | bytes 98312 | tf_op jit(solution)/shard_map/ppermute | solution.py:383
  17.4 1.0 %copy-start = (f32[64,2048]{1,0:T(8,128)S(1)}, f32[64,2048]{1,0:T(8,128)}, u32[]{:S(2)}) copy-start(f32[64,2048]{1,0:T(8,128)} %factor_ref.3) | copy-start | bytes 1572868
  18.4 0.8 %copy-start.3 = (f32[32,512]{1,0:T(8,128)S(1)}, f32[32,512]{1,0:T(8,128)}, u32[]{:S(2)}) copy-start(f32[32,512]{1,0:T(8,128)} %rhs_ref.3) | copy-start | bytes 196612
  18.4 11.6 %copy-start.1 = (f32[64,2048]{1,0:T(8,128)S(1)}, f32[64,2048]{1,0:T(8,128)}, u32[]{:S(2)}) copy-start(f32[64,2048]{1,0:T(8,128)} %factor_ref.3) | copy-start | bytes 1572868
  18.7 1.5 %collective-permute-start = (f32[8,128]{1,0:T(8,128)S(1)}, f32[8,128]{1,0:T(8,128)S(1)}, u32[]{:S(2)}, u32[]{:S(2)}) collective-permute-start(f32[8,128]{1,0:T(8,128)S(1)} %get-tuple-element.19), channel_id=1, source_target_pairs={{0,16},{16,0},{1,17},{17,1},{2,18},{18,2},{3,19},{19,3},{4,20},{20... | collective-permute-start | bytes 12296 | tf_op jit(solution)/shard_map/ppermute | solution.py:398
  31.1 9.6 %all-to-all-start.2 = ((f32[32,1,128]{2,1,0:T(1,128)}), f32[32,1,128]{2,1,0:T(1,128)S(1)}, u32[]{:S(2)}, u32[]{:S(2)}) async-start(f32[32,1,128]{2,1,0:T(1,128)} %bitcast.5), calls=%async_computation.2 | async-start | bytes 32768 | tf_op jit(solution)/shard_map/all_to_all | solution.py:375

commit v3 on v2

--- a/solution.py
+++ b/solution.py
@@ -65,27 +65,39 @@
     return parts
 
 
-def start_kernel(grid, rhs_ref, diag_ref, slots_ref, edge_a_ref, edge_b_ref):
+def start_kernel(
+    grid, rhs_in, diag_in, factor_in, slots_ref, rhs_ref, diag_ref, factor_ref, *rest
+):
+    edge_refs, sems = rest[:-1], rest[-1]
+    loads = [
+        pltpu.make_async_copy(source, target, sems.at[k])
+        for k, (source, target) in enumerate(
+            ((rhs_in, rhs_ref), (diag_in, diag_ref), (factor_in, factor_ref))
+        )
+    ]
+    for load in loads:
+        load.start()
     groups, tiles = grid
     g, t = lax.axis_index("grp"), lax.axis_index("tile")
     rows, cols = rhs_ref.shape
     count = groups * tiles
     per_row = cols // FAC
     even = lax.rem(g, 2) == 0
+    pick = (
+        lax.broadcasted_iota(jnp.int32, (cols, LANES), 0) // FAC
+        == lax.rem(lane_iota((cols, LANES)), per_row)
+    ).astype(jnp.float32)
+    loads[0].wait()
+    loads[1].wait()
     for at, ref in ((0, rhs_ref), (HALO, diag_ref)):
         first, last = ref[:HALO, :], ref[rows - HALO :, :]
-        edge_a_ref[at : at + HALO, :] = jnp.where(even, last, first)
-        if groups > 2:
-            edge_b_ref[at : at + HALO, :] = jnp.where(even, first, last)
+        for edge_ref, odd in zip(edge_refs, (False, True)):
+            edge_ref[at : at + HALO, :] = jnp.where(even != odd, last, first)
     sums = []
     for ref in (rhs_ref, diag_ref):
         for a in range(rows // FAC):
             sums.append(jnp.sum(ref[a * FAC : (a + 1) * FAC, :], axis=0, keepdims=True))
     tall = jnp.concatenate(sums + [jnp.zeros((SUB - len(sums), cols), jnp.float32)], axis=0)
-    pick = (
-        lax.broadcasted_iota(jnp.int32, (cols, LANES), 0) // FAC
-        == lax.rem(lane_iota((cols, LANES)), per_row)
-    ).astype(jnp.float32)
     means = jnp.dot(
         tall, pick, precision=lax.Precision.HIGHEST, preferred_element_type=jnp.float32
     ) * (1.0 / (FAC * FAC))
@@ -102,6 +114,7 @@
     lines.append(jnp.broadcast_to(coarse, (count, LANES)))
     for k, line in enumerate(lines):
         slots_ref[pl.ds(k, count, stride=len(lines)), :] = line
+    loads[2].wait()
 
 
 def two_products(vector, factor_ref):
@@ -377,14 +390,26 @@
 
     width = 2 * rows * HALO // LANES + 1
     edge = (2 * HALO, cols)
-    slots, edge_a, edge_b = call(
-        functools.partial(start_kernel, grid), [(count * width, LANES), edge, edge], 2
-    )(right_side, diagonal)
-    near = lax.ppermute(edge_a, "grp", swap)
+    shapes = [(count * width, LANES), (rows, cols), (rows, cols), inverse_factor.shape]
+    shapes += [edge] * (2 if groups > 2 else 1)
+    slots, right_side, diagonal, inverse_factor, *edges = pl.pallas_call(
+        functools.partial(start_kernel, grid),
+        out_shape=[jax.ShapeDtypeStruct(s, jnp.float32) for s in shapes],
+        in_specs=[pl.BlockSpec(memory_space=pltpu.HBM)] * 3,
+        out_specs=[VMEM] * len(shapes),
+        scratch_shapes=[pltpu.SemaphoreType.DMA((3,))],
+        compiler_params=pltpu.CompilerParams(vmem_limit_bytes=LIMIT),
+    )(
+        *[
+            pltpu.with_memory_space_constraint(x, pltpu.HBM)
+            for x in (right_side, diagonal, inverse_factor)
+        ]
+    )
+    near = lax.ppermute(edges[0], "grp", swap)
     if groups > 2:
         across = [(i, i + 1) for i in range(1, groups - 1, 2)]
         across += [(j, i) for i, j in across]
-        far = lax.ppermute(edge_b, "grp", across)
+        far = lax.ppermute(edges[1], "grp", across)
         below = jnp.where(g % 2 == 0, near, far)
         above = jnp.where(g % 2 == 0, far, near)
     else:

time: 41.8 us -> 39.6 us (0.947)
  local copies, waits for them, and re-layouts: 3.25 us -> 0 us
  Pallas kernels: 4.29 us -> 5.17 us
    unnamed x12 -> x0, local copies, waits for them, and re-layouts: 3.25 us -> none
    pallas_call x1, Pallas kernels: 0.9 us -> 1.78 us  [shards(): pl.pallas_call(functools.partial(start_kernel, grid), out_shape=[jax.Shap...]
  transfers between devices with their start and end apart: 4 -> 4, of which waited for: 2 -> 3; matrix products, arithmetic and copies ran while one was open for 0% -> 0% of each run, Pallas kernels for 4% -> 4%
where the time goes in v3:
time: 39.6 us; the launch traced here: 39.4 us
  waiting for transfers between devices  13.9 us (35%)
  starting transfers between devices  10.3 us (26%)
  blocking collectives  9.93 us (25%)
  Pallas kernels  5.17 us (13%)
    all_to_all x2, waiting for transfers between devices, exchange(): lax.all_to_all(slots.reshape(count, lines * LANES), everyone, 0, 0, tiled...  13.6 us
    all_to_all x1, blocking collectives, exchange(): lax.all_to_all(slots.reshape(count, lines * LANES), everyone, 0, 0, tiled...  9.93 us
    all_to_all x2, starting transfers between devices, exchange(): lax.all_to_all(slots.reshape(count, lines * LANES), everyone, 0, 0, tiled...  9.88 us
    pallas_call x1, Pallas kernels, shards(): pl.pallas_call(functools.partial(start_kernel, grid), out_shape=[jax.Shap...  1.78 us
    pallas_call x1, Pallas kernels, shards(): call(functools.partial(second_kernel, grid, blocks), [(high, LANES), (cou...  0.99 us
    pallas_call x1, Pallas kernels, shards(): call(functools.partial(smooth_kernel, grid, width), [wide] * 4 + [(SUB, L...  0.83 us
  transfers between devices with their start and end apart: 4, of which 3 were waited for; matrix products, arithmetic and copies ran while one was open for 0% of the time, Pallas kernels for 4%

profile of v3, /device:TPU:0, one launch (start us, length us, event | category | flops | bytes accessed | tf_op | source)
XLA Modules:
  0.0 39.4 jit_solution(11987929872288037809)
XLA Ops:
  0.0 1.8 %shard_map.37 = (f32[160,128]{1,0:T(8,128)}, f32[32,512]{1,0:T(8,128)S(1)}, f32[32,512]{1,0:T(8,128)S(1)}, f32[64,2048]{1,0:T(8,128)S(1)}, f32[16,512]{1,0:T(8,128)S(1)}) custom-call(f32[32,512]{1,0:T(8,128)} %rhs_in.1, f32[32,512]{1,0:T(8,128)} %diag_in.1, f32[64,2048]{1,0:T(8,128)} %factor_in.1), custom_call_target="tpu_custom_call" | custom-call | tf_op jit(solution)/shard_map/pallas_call | solution.py:395
  1.8 7.3 %all-to-all-start = ((f32[32,1,640]{2,1,0:T(1,128)}), f32[32,1,640]{2,1,0:T(1,128)S(1)}, u32[]{:S(2)}, u32[]{:S(2)}) async-start(f32[32,1,640]{2,1,0:T(1,128)} %bitcast), calls=%async_computation | async-start | bytes 163840 | tf_op jit(solution)/shard_map/all_to_all | solution.py:388
  9.1 0.3 collective-permute-start.1
  9.4 7.2 %all-to-all-done = f32[32,1,640]{2,1,0:T(1,128)S(1)} async-done(((f32[32,1,640]{2,1,0:T(1,128)}), f32[32,1,640]{2,1,0:T(1,128)S(1)}, u32[]{:S(2)}, u32[]{:S(2)}) %all-to-all-start) | async-done | bytes 81952 | tf_op jit(solution)/shard_map/all_to_all | solution.py:388
  16.6 0.2 shard_map.38
  16.8 0.1 collective-permute-start
  16.9 0.0 collective-permute-done.1.below_ref.above_ref
  16.9 0.8 %shard_map.39 = (f32[48,640]{1,0:T(8,128)S(1)}, f32[48,640]{1,0:T(8,128)S(1)}, f32[48,640]{1,0:T(8,128)S(1)}, f32[48,640]{1,0:T(8,128)S(1)}, f32[8,128]{1,0:T(8,128)S(1)}) custom-call(f32[160,128]{1,0:T(8,128)S(1)} %bitcast.9, f32[32,512]{1,0:T(8,128)S(1)} %get-tuple-element.24.rhs_ref, f32[32,512]{1,0:T(8,128)S(1)} %get-tuple-element.25.diag_ref, ...), custom_call_target="tpu_custom_call" | custom-call | tf_op jit(solution)/shard_map/pallas_call | solution.py:425
  17.7 0.3 collective-permute-done.came_ref
  18.1 9.9 %all_to_all.29 = f32[32,1,1152]{2,1,0:T(1,128)S(1)} all-to-all(f32[32,1,1152]{2,1,0:T(1,128)S(1)} %bitcast.10), channel_id=1, replica_groups=mesh['grp'=2,'tile'=16] {'grp','tile'}, dimensions={0} | all-to-all | bytes 294912 | tf_op jit(solution)/shard_map/all_to_all | solution.py:388
  28.0 1.0 %shard_map.41 = (f32[16,128]{1,0:T(8,128)S(1)}, f32[32,128]{1,0:T(8,128)}) custom-call(f32[288,128]{1,0:T(8,128)S(1)} %bitcast.11, f32[16,128]{1,0:T(8,128)S(1)} %get-tuple-element.28.mean_ref, f32[64,2048]{1,0:T(8,128)S(1)} %get-tuple-element.21.factor_ref), custom_call_target="tpu_custom_call" | custom-call | tf_op jit(solution)/shard_map/pallas_call | solution.py:431
  29.0 2.5 %all-to-all-start.2 = ((f32[32,1,128]{2,1,0:T(1,128)}), f32[32,1,128]{2,1,0:T(1,128)S(1)}, u32[]{:S(2)}, u32[]{:S(2)}) async-start(f32[32,1,128]{2,1,0:T(1,128)} %bitcast.5), calls=%async_computation.2 | async-start | bytes 32768 | tf_op jit(solution)/shard_map/all_to_all | solution.py:388
  31.6 0.6 %shard_map.42.base_ref = f32[32,512]{1,0:T(8,128)S(1)} custom-call(f32[16,128]{1,0:T(8,128)S(1)} %get-tuple-element.30.value_ref, f32[48,640]{1,0:T(8,128)S(1)} %get-tuple-element.31.rhs_ref, f32[48,640]{1,0:T(8,128)S(1)} %get-tuple-element.32.diag_ref, f32[48,640]{1,0:T(8,128)S(1)} %get-tuple-element.33.weight_ref, f32[48,640]{1,0:T(8,128)S(1)} %get-tuple-element.34.smooth_ref), custom_call_target="tpu_custom_call" | custom-call | tf_op jit(solution)/shard_map/pallas_call | solution.py:435
  32.2 6.5 %all-to-all-done.2 = f32[32,1,128]{2,1,0:T(1,128)S(1)} async-done(((f32[32,1,128]{2,1,0:T(1,128)}), f32[32,1,128]{2,1,0:T(1,128)S(1)}, u32[]{:S(2)}, u32[]{:S(2)}) %all-to-all-start.2) | async-done | bytes 16416 | tf_op jit(solution)/shard_map/all_to_all | solution.py:388
  38.6 0.7 %shard_map.43 = f32[32,512]{1,0:T(8,128)} custom-call(f32[32,128]{1,0:T(8,128)S(1)} %bitcast.12, f32[32,512]{1,0:T(8,128)S(1)} %shard_map.42.base_ref), custom_call_target="tpu_custom_call" | custom-call | tf_op jit(solution)/shard_map/pallas_call | solution.py:438
  (1 shorter events, 0.0 us)
Async XLA Ops:
  1.8 14.8 %all-to-all-start = ((f32[32,1,640]{2,1,0:T(1,128)}), f32[32,1,640]{2,1,0:T(1,128)S(1)}, u32[]{:S(2)}, u32[]{:S(2)}) async-start(f32[32,1,640]{2,1,0:T(1,128)} %bitcast), calls=%async_computation | async-start | bytes 163840 | tf_op jit(solution)/shard_map/all_to_all | solution.py:388
  9.1 7.8 %collective-permute-start.1 = (f32[16,512]{1,0:T(8,128)S(1)}, f32[16,512]{1,0:T(8,128)S(1)}, u32[]{:S(2)}, u32[]{:S(2)}) collective-permute-start(f32[16,512]{1,0:T(8,128)S(1)} %get-tuple-element.26), channel_id=1, source_target_pairs={{0,16},{16,0},{1,17},{17,1},{2,18},{18,2},{3,19},{19,3},{4,20},{20... | collective-permute-start | bytes 98312 | tf_op jit(solution)/shard_map/ppermute | solution.py:408
  16.8 1.2 %collective-permute-start = (f32[8,128]{1,0:T(8,128)S(1)}, f32[8,128]{1,0:T(8,128)S(1)}, u32[]{:S(2)}, u32[]{:S(2)}) collective-permute-start(f32[8,128]{1,0:T(8,128)S(1)} %get-tuple-element.23), channel_id=1, source_target_pairs={{0,16},{16,0},{1,17},{17,1},{2,18},{18,2},{3,19},{19,3},{4,20},{20... | collective-permute-start | bytes 12296 | tf_op jit(solution)/shard_map/ppermute | solution.py:423
  29.0 9.6 %all-to-all-start.2 = ((f32[32,1,128]{2,1,0:T(1,128)}), f32[32,1,128]{2,1,0:T(1,128)S(1)}, u32[]{:S(2)}, u32[]{:S(2)}) async-start(f32[32,1,128]{2,1,0:T(1,128)} %bitcast.5), calls=%async_computation.2 | async-start | bytes 32768 | tf_op jit(solution)/shard_map/all_to_all | solution.py:388

commit v4 on v3

--- a/solution.py
+++ b/solution.py
@@ -51,6 +51,37 @@
 
 def gather_lanes(x, index):
     return jnp.take_along_axis(x, index, axis=1)
+
+
+def block_means(arrays):
+    rows, cols = arrays[0].shape
+    per_row = cols // FAC
+    sums = [
+        jnp.sum(x[a * FAC : (a + 1) * FAC], axis=0, keepdims=True)
+        for x in arrays
+        for a in range(rows // FAC)
+    ]
+    used = len(sums)
+    high = jnp.concatenate(sums, axis=0)
+    parts = []
+    for _ in range(3):
+        part = high.astype(jnp.bfloat16)
+        parts.append(part.astype(jnp.float32))
+        high = high - parts[-1]
+    fill = -len(parts) * used % (2 * SUB)
+    tall = jnp.concatenate(parts + [jnp.zeros((fill, cols), jnp.float32)], axis=0)
+    pick = (
+        lax.broadcasted_iota(jnp.int32, (cols, LANES), 0) // FAC
+        == lax.rem(lane_iota((cols, LANES)), per_row)
+    )
+    line = jnp.dot(
+        tall.astype(jnp.bfloat16),
+        pick.astype(jnp.bfloat16),
+        preferred_element_type=jnp.float32,
+    )
+    mine = lax.rem(row_iota(line.shape), used) == lax.rem(lane_iota(line.shape) // per_row, used)
+    line = jnp.where(mine, line, 0.0)
+    return jnp.sum(line, axis=0, keepdims=True) * (1.0 / (FAC * FAC))
 
 
 def pack_lanes(strip, first):
@@ -81,30 +112,14 @@
     g, t = lax.axis_index("grp"), lax.axis_index("tile")
     rows, cols = rhs_ref.shape
     count = groups * tiles
-    per_row = cols // FAC
     even = lax.rem(g, 2) == 0
-    pick = (
-        lax.broadcasted_iota(jnp.int32, (cols, LANES), 0) // FAC
-        == lax.rem(lane_iota((cols, LANES)), per_row)
-    ).astype(jnp.float32)
     loads[0].wait()
     loads[1].wait()
     for at, ref in ((0, rhs_ref), (HALO, diag_ref)):
         first, last = ref[:HALO, :], ref[rows - HALO :, :]
         for edge_ref, odd in zip(edge_refs, (False, True)):
             edge_ref[at : at + HALO, :] = jnp.where(even != odd, last, first)
-    sums = []
-    for ref in (rhs_ref, diag_ref):
-        for a in range(rows // FAC):
-            sums.append(jnp.sum(ref[a * FAC : (a + 1) * FAC, :], axis=0, keepdims=True))
-    tall = jnp.concatenate(sums + [jnp.zeros((SUB - len(sums), cols), jnp.float32)], axis=0)
-    means = jnp.dot(
-        tall, pick, precision=lax.Precision.HIGHEST, preferred_element_type=jnp.float32
-    ) * (1.0 / (FAC * FAC))
-    group_of = lane_iota((1, LANES)) // per_row
-    coarse = jnp.zeros((1, LANES), jnp.float32)
-    for k in range(LANES // per_row):
-        coarse = jnp.where(group_of == k, means[k : k + 1, :], coarse)
+    coarse = block_means([rhs_ref[...], diag_ref[...]])
     to_left = lax.rem(row_iota((count, LANES)), tiles) < t
     lines = []
     for ref in (rhs_ref, diag_ref):
@@ -216,23 +231,7 @@
         smooth = (1.0 - OMEGA) * smooth + weight * (rhs + neighbour_sum(smooth))
     smooth_out[...] = smooth
     left_over = (rhs - (6.0 + diag) * smooth + neighbour_sum(smooth))[:rows, :cols]
-    per_row = cols // FAC
-    sums = [
-        jnp.sum(left_over[a * FAC : (a + 1) * FAC], axis=0, keepdims=True)
-        for a in range(rows // FAC)
-    ]
-    tall = jnp.concatenate(sums + [jnp.zeros((SUB - len(sums), cols), jnp.float32)], axis=0)
-    pick = (
-        lax.broadcasted_iota(jnp.int32, (cols, LANES), 0) // FAC
-        == lax.rem(lane_iota((cols, LANES)), per_row)
-    ).astype(jnp.float32)
-    means = jnp.dot(
-        tall, pick, precision=lax.Precision.HIGHEST, preferred_element_type=jnp.float32
-    ) * (1.0 / (FAC * FAC))
-    group_of = lax.rem(lane_iota((1, LANES)) // per_row, rows // FAC)
-    coarse = jnp.zeros((1, LANES), jnp.float32)
-    for a in range(rows // FAC):
-        coarse = jnp.where(group_of == a, means[a : a + 1, :], coarse)
+    coarse = block_means([left_over])
     coarse_out[...] = jnp.broadcast_to(coarse, (SUB, LANES))
 
 
@@ -312,12 +311,12 @@
     return gather_lanes(jnp.broadcast_to(line, shape), index)
 
 
-def resmooth_kernel(
-    grid, value_ref, rhs_ref, diag_ref, weight_ref, smooth_ref, base_ref, field_ref
+def last_kernel(
+    grid, got_ref, value_ref, rhs_ref, diag_ref, weight_ref, smooth_ref, out_ref, field_ref
 ):
     groups, tiles = grid
     g, t = lax.axis_index("grp"), lax.axis_index("tile")
-    rows, cols = base_ref.shape
+    rows, cols = out_ref.shape
     block_rows, per_row = rows // FAC, cols // FAC
     here = block_rows * per_row
     inside = inside_mask(grid, rows, cols)
@@ -356,19 +355,14 @@
     smooth = weight * rest
     for _ in range(SWEEPS - 1):
         smooth = (1.0 - OMEGA) * smooth + weight * (rest + neighbour_sum(smooth))
-    base_ref[...] = field[:rows, :cols] + smooth[:rows, :cols]
-
-
-def last_kernel(got_ref, base_ref, out_ref):
-    rows, cols = out_ref.shape
-    per_row = cols // FAC
+    base = field[:rows, :cols] + smooth[:rows, :cols]
     line = MIX * jnp.sum(got_ref[...], axis=0, keepdims=True)
     for a in range(rows // FAC):
         for q in range(cols // LANES):
             part = prolong_line(line, a * per_row + q * (LANES // FAC), (SUB, LANES))
             for low in range(a * FAC, (a + 1) * FAC, SUB):
                 where = (slice(low, low + SUB), slice(q * LANES, (q + 1) * LANES))
-                out_ref[where] = base_ref[where] + part
+                out_ref[where] = base[where] + part
 
 
 def shards(right_side, diagonal, inverse_factor):
@@ -405,6 +399,8 @@
             for x in (right_side, diagonal, inverse_factor)
         ]
     )
+    got = exchange(slots)
+    got, edges = lax.optimization_barrier((got, edges))
     near = lax.ppermute(edges[0], "grp", swap)
     if groups > 2:
         across = [(i, i + 1) for i in range(1, groups - 1, 2)]
@@ -414,7 +410,6 @@
         above = jnp.where(g % 2 == 0, far, near)
     else:
         below, above = near, near
-    got = exchange(slots)
 
     half = (high // 2, LANES)
     keep, send, mean = call(
@@ -432,10 +427,9 @@
         functools.partial(second_kernel, grid, blocks), [(high, LANES), (count, LANES)], 3
     )(got, mean, inverse_factor)
     got = exchange(slots)
-    (base,) = call(
-        functools.partial(resmooth_kernel, grid), [(rows, cols)], 5, [wide]
-    )(value, rhs, diag, weight, smooth)
-    (field,) = call(last_kernel, [(rows, cols)], 2)(got, base)
+    (field,) = call(
+        functools.partial(last_kernel, grid), [(rows, cols)], 6, [wide]
+    )(got, value, rhs, diag, weight, smooth)
     return field
 
 

time: 39.6 us -> 38.6 us (0.975)
  blocking collectives: 9.93 us -> 33.6 us
  waiting for transfers between devices: 13.9 us -> 0.42 us
  starting transfers between devices: 10.3 us -> 0.57 us
  Pallas kernels: 5.17 us -> 3.75 us
    all_to_all x1 -> x3, blocking collectives: 9.93 us -> 33.6 us  [exchange(): lax.all_to_all(slots.reshape(count, lines * LANES), everyone, 0, 0, tiled...]
    all_to_all x2 -> x0, waiting for transfers between devices: 13.6 us -> none  [exchange(): lax.all_to_all(slots.reshape(count, lines * LANES), everyone, 0, 0, tiled...]
    all_to_all x2 -> x0, starting transfers between devices: 9.88 us -> none  [exchange(): lax.all_to_all(slots.reshape(count, lines * LANES), everyone, 0, 0, tiled...]
    pallas_call x1, Pallas kernels: 1.78 us -> 1.14 us  [shards(): pl.pallas_call(functools.partial(start_kernel, grid), out_shape=[jax.Shap...]
    pallas_call x1, Pallas kernels: 0.99 us -> 0.38 us  [shards(): call(functools.partial(second_kernel, grid, blocks), [(high, LANES), (cou...]
    ppermute x1, starting transfers between devices: 0.07 us -> 0.57 us  [shards(): came = lax.ppermute(send, 'grp', swap)]
    ppermute x1, waiting for transfers between devices: 0.01 us -> 0.41 us  [shards(): near = lax.ppermute(edges[0], 'grp', swap)]
    pallas_call x2 -> x1, Pallas kernels: 1.34 us -> 1.24 us  [shards(): call(functools.partial(last_kernel, grid), [(rows, cols)], 6, [wide])]
  transfers between devices with their start and end apart: 4 -> 2, of which waited for: 3 -> 1; matrix products, arithmetic and copies ran while one was open for 0% -> 0% of each run, Pallas kernels for 4% -> 2%
where the time goes in v4:
time: 38.6 us; the launch traced here: 38.4 us
  blocking collectives  33.6 us (87%)
  Pallas kernels  3.75 us (10%)
  starting transfers between devices  0.57 us (1%)
  waiting for transfers between devices  0.42 us (1%)
    all_to_all x3, blocking collectives, exchange(): lax.all_to_all(slots.reshape(count, lines * LANES), everyone, 0, 0, tiled...  33.6 us
    pallas_call x1, Pallas kernels, shards(): call(functools.partial(last_kernel, grid), [(rows, cols)], 6, [wide])  1.24 us
    pallas_call x1, Pallas kernels, shards(): pl.pallas_call(functools.partial(start_kernel, grid), out_shape=[jax.Shap...  1.14 us
  transfers between devices with their start and end apart: 2, of which 1 were waited for; matrix products, arithmetic and copies ran while one was open for 0% of the time, Pallas kernels for 2%

profile of v4, /device:TPU:0, one launch (start us, length us, event | category | flops | bytes accessed | tf_op | source)
XLA Modules:
  0.0 38.4 jit_solution(8092430024109756833)
XLA Ops:
  0.0 1.1 %shard_map.37 = (f32[160,128]{1,0:T(8,128)S(1)}, f32[32,512]{1,0:T(8,128)S(1)}, f32[32,512]{1,0:T(8,128)S(1)}, f32[64,2048]{1,0:T(8,128)S(1)}, f32[16,512]{1,0:T(8,128)S(1)}) custom-call(f32[32,512]{1,0:T(8,128)} %rhs_in.1, f32[32,512]{1,0:T(8,128)} %diag_in.1, f32[64,2048]{1,0:T(8,128)} %factor_in.1), custom_call_target="tpu_custom_call" | custom-call | tf_op jit(solution)/shard_map/pallas_call | solution.py:389
  1.2 14.6 %all_to_all.29 = f32[32,1,640]{2,1,0:T(1,128)S(1)} all-to-all(f32[32,1,640]{2,1,0:T(1,128)S(1)} %bitcast.12), channel_id=1, replica_groups=mesh['grp'=2,'tile'=16] {'grp','tile'}, dimensions={0} | all-to-all | bytes 163840 | tf_op jit(solution)/shard_map/all_to_all | solution.py:382
  15.8 0.0 collective-permute-start.1
  15.8 0.2 shard_map.38
  16.0 0.6 %collective-permute-start = (f32[8,128]{1,0:T(8,128)S(1)}, f32[8,128]{1,0:T(8,128)S(1)}, u32[]{:S(2)}, u32[]{:S(2)}) collective-permute-start(f32[8,128]{1,0:T(8,128)S(1)} %get-tuple-element.27), channel_id=1, source_target_pairs={{0,16},{16,0},{1,17},{17,1},{2,18},{18,2},{3,19},{19,3},{4,20},{20... | collective-permute-start | bytes 12296 | tf_op jit(solution)/shard_map/ppermute | solution.py:418
  16.5 0.4 %collective-permute-done.1.below_ref.above_ref = f32[16,512]{1,0:T(8,128)S(1)} collective-permute-done((f32[16,512]{1,0:T(8,128)S(1)}, f32[16,512]{1,0:T(8,128)S(1)}, u32[]{:S(2)}, u32[]{:S(2)}) %collective-permute-start.1) | collective-permute-done | bytes 32800 | tf_op jit(solution)/shard_map/ppermute | solution.py:404
  17.0 0.7 %shard_map.39 = (f32[48,640]{1,0:T(8,128)S(1)}, f32[48,640]{1,0:T(8,128)S(1)}, f32[48,640]{1,0:T(8,128)S(1)}, f32[48,640]{1,0:T(8,128)S(1)}, f32[8,128]{1,0:T(8,128)S(1)}) custom-call(f32[160,128]{1,0:T(8,128)S(1)} %bitcast.9, f32[32,512]{1,0:T(8,128)S(1)} %get-tuple-element.28.rhs_ref, f32[32,512]{1,0:T(8,128)S(1)} %get-tuple-element.29.diag_ref, ...), custom_call_target="tpu_custom_call" | custom-call | tf_op jit(solution)/shard_map/pallas_call | solution.py:420
  17.7 0.0 collective-permute-done.came_ref
  17.7 9.9 %all_to_all.30 = f32[32,1,1152]{2,1,0:T(1,128)S(1)} all-to-all(f32[32,1,1152]{2,1,0:T(1,128)S(1)} %bitcast.10), channel_id=1, replica_groups=mesh['grp'=2,'tile'=16] {'grp','tile'}, dimensions={0} | all-to-all | bytes 294912 | tf_op jit(solution)/shard_map/all_to_all | solution.py:382
  27.7 0.4 shard_map.41
  28.1 9.1 %all_to_all.31 = f32[32,1,128]{2,1,0:T(1,128)S(1)} all-to-all(f32[32,1,128]{2,1,0:T(1,128)S(1)} %bitcast.14), channel_id=1, replica_groups=mesh['grp'=2,'tile'=16] {'grp','tile'}, dimensions={0} | all-to-all | bytes 32768 | tf_op jit(solution)/shard_map/all_to_all | solution.py:382
  37.1 1.2 %shard_map.42 = f32[32,512]{1,0:T(8,128)} custom-call(f32[32,128]{1,0:T(8,128)S(1)} %bitcast.13, f32[16,128]{1,0:T(8,128)S(1)} %get-tuple-element.34.value_ref, f32[48,640]{1,0:T(8,128)S(1)} %get-tuple-element.35.rhs_ref, f32[48,640]{1,0:T(8,128)S(1)} %get-tuple-element.36.diag_ref, f32[48,640]{1,0:T(8,128)S(1)} %get-tuple-element.37.weight_ref, ...), custom_call_target="tpu_custom_call" | custom-call | tf_op jit(solution)/shard_map/pallas_call | solution.py:430
  (1 shorter events, 0.0 us)
Async XLA Ops:
  15.8 1.2 %collective-permute-start.1 = (f32[16,512]{1,0:T(8,128)S(1)}, f32[16,512]{1,0:T(8,128)S(1)}, u32[]{:S(2)}, u32[]{:S(2)}) collective-permute-start(f32[16,512]{1,0:T(8,128)S(1)} %get-tuple-element.30), channel_id=1, source_target_pairs={{0,16},{16,0},{1,17},{17,1},{2,18},{18,2},{3,19},{19,3},{4,20},{20... | collective-permute-start | bytes 98312 | tf_op jit(solution)/shard_map/ppermute | solution.py:404
  16.0 1.7 %collective-permute-start = (f32[8,128]{1,0:T(8,128)S(1)}, f32[8,128]{1,0:T(8,128)S(1)}, u32[]{:S(2)}, u32[]{:S(2)}) collective-permute-start(f32[8,128]{1,0:T(8,128)S(1)} %get-tuple-element.27), channel_id=1, source_target_pairs={{0,16},{16,0},{1,17},{17,1},{2,18},{18,2},{3,19},{19,3},{4,20},{20... | collective-permute-start | bytes 12296 | tf_op jit(solution)/shard_map/ppermute | solution.py:418

commit v5 on v4

--- a/solution.py
+++ b/solution.py
@@ -6,6 +6,7 @@
 from jax.experimental import pallas as pl
 from jax.experimental.pallas import tpu as pltpu
 from jax.sharding import PartitionSpec as P
+
 
 FAC = 16
 SWEEPS = 4
@@ -18,17 +19,18 @@
 VMEM = pl.BlockSpec(memory_space=pltpu.VMEM)
 
 
-LIMIT = 8 * 1024 * 1024
-
-
-def call(body, shapes, count, scratch=()):
+def limit(points):
+    return 4 * 1024 * 1024 + 2048 * points
+
+
+def call(points, body, shapes, count, scratch=()):
     return pl.pallas_call(
         body,
         out_shape=[jax.ShapeDtypeStruct(s, jnp.float32) for s in shapes],
         in_specs=[VMEM] * count,
         out_specs=[VMEM] * len(shapes),
         scratch_shapes=[pltpu.VMEM(s, jnp.float32) for s in scratch],
-        compiler_params=pltpu.CompilerParams(vmem_limit_bytes=LIMIT),
+        compiler_params=pltpu.CompilerParams(vmem_limit_bytes=limit(points)),
     )
 
 
@@ -97,9 +99,11 @@
 
 
 def start_kernel(
-    grid, rhs_in, diag_in, factor_in, slots_ref, rhs_ref, diag_ref, factor_ref, *rest
+    grid, rhs_in, diag_in, factor_in, slots_ref, rhs_ref, diag_ref, mine_ref, *rest
 ):
     edge_refs, sems = rest[:-1], rest[-1]
+    here = factor_in.shape[0]
+    factor_ref = mine_ref.at[:here, :]
     loads = [
         pltpu.make_async_copy(source, target, sems.at[k])
         for k, (source, target) in enumerate(
@@ -115,10 +119,11 @@
     even = lax.rem(g, 2) == 0
     loads[0].wait()
     loads[1].wait()
-    for at, ref in ((0, rhs_ref), (HALO, diag_ref)):
+    for at, ref in ((0, rhs_ref), (cols, diag_ref)):
         first, last = ref[:HALO, :], ref[rows - HALO :, :]
-        for edge_ref, odd in zip(edge_refs, (False, True)):
-            edge_ref[at : at + HALO, :] = jnp.where(even != odd, last, first)
+        mine_ref[here:, at : at + cols] = jnp.where(even, last, first)
+        for edge_ref in edge_refs:
+            edge_ref[:, at : at + cols] = jnp.where(even, first, last)
     coarse = block_means([rhs_ref[...], diag_ref[...]])
     to_left = lax.rem(row_iota((count, LANES)), tiles) < t
     lines = []
@@ -132,17 +137,12 @@
     loads[2].wait()
 
 
-def two_products(vector, factor_ref):
-    high = factor_ref.shape[1] // LANES
+def products(vector, factor_ref, here):
     total = None
-    for m in range(high):
-        term = factor_ref[:, m * LANES : (m + 1) * LANES] * vector[m : m + 1, :]
+    for m in range(vector.shape[0]):
+        term = factor_ref[:here, m * LANES : (m + 1) * LANES] * vector[m : m + 1, :]
         total = term if total is None else total + term
-    inner = jnp.sum(total, axis=1, keepdims=True)
-    return [
-        jnp.sum(factor_ref[:, m * LANES : (m + 1) * LANES] * inner, axis=0, keepdims=True)
-        for m in range(high)
-    ]
+    return jnp.sum(total, axis=1, keepdims=True)
 
 
 def interleave(even, odd):
@@ -154,19 +154,6 @@
     return [
         ref[pl.ds(line + side * width, count // 2, stride=2 * width), :] for side in range(2)
     ]
-
-
-def first_kernel(width, got_ref, factor_ref, keep_ref, send_ref, mean_ref):
-    high = factor_ref.shape[1] // LANES
-    even, odd = pairs(got_ref, width - 1, width)
-    half = LANES // 2
-    mean_ref[...] = interleave(shift(even, half, 1), odd)
-    terms = two_products(interleave(even, shift(odd, half, 1)), factor_ref)
-    own = lax.rem(lax.axis_index("grp"), 2) == 0
-    for m in range(high // 2):
-        low, top = terms[m], terms[m + high // 2]
-        keep_ref[m : m + 1, :] = jnp.where(own, low, top)
-        send_ref[m : m + 1, :] = jnp.where(own, top, low)
 
 
 def inside_mask(grid, rows, cols):
@@ -194,21 +181,43 @@
     return jnp.concatenate(parts, axis=0)
 
 
-def smooth_kernel(
-    grid, width, got_ref, rhs_ref, diag_ref, below_ref, above_ref,
-    rhs_out, diag_out, weight_out, smooth_out, coarse_out,
+def middle_kernel(
+    grid, width, got_ref, rhs_ref, diag_ref, mine_ref, theirs_ref, *refs
 ):
+    far_refs, (rhs_out, diag_out, weight_out, smooth_out, mean_ref, slots_ref, half_ref) = (
+        refs[:-7],
+        refs[-7:],
+    )
     groups, tiles = grid
     g, t = lax.axis_index("grp"), lax.axis_index("tile")
     rows, cols = rhs_ref.shape
+    here = mine_ref.shape[0] - HALO
+    high = half_ref.shape[0]
+    even, odd = pairs(got_ref, width - 1, width)
+    mean_ref[...] = interleave(shift(even, LANES // 2, 1), odd)
+    vector = interleave(even, shift(odd, LANES // 2, 1))
+    inner = products(vector, mine_ref, here)
+    other = products(vector, theirs_ref, here)
+    start = lax.rem(g, 2) * (high * LANES)
+    for m in range(high):
+        place = pl.ds(pl.multiple_of(start + m * LANES, LANES), LANES)
+        term = mine_ref[:here, place] * inner + theirs_ref[:here, place] * other
+        half_ref[m : m + 1, :] = jnp.sum(term, axis=0, keepdims=True)
+    near_ref = theirs_ref.at[here:, :]
+    if groups > 2:
+        near, far = near_ref[:, : 2 * cols], far_refs[0][...]
+        is_even = lax.rem(g, 2) == 0
+        below, above = jnp.where(is_even, near, far), jnp.where(is_even, far, near)
+    else:
+        below = above = near_ref[:, : 2 * cols]
     up, down = jnp.maximum(g - 1, 0), jnp.minimum(g + 1, groups - 1)
     left, right = jnp.maximum(t - 1, 0), jnp.minimum(t + 1, tiles - 1)
     inside = inside_mask(grid, rows, cols)
     at = 0
-    for ref, out, edge in ((rhs_ref, rhs_out, 0), (diag_ref, diag_out, HALO)):
+    for ref, out, edge in ((rhs_ref, rhs_out, 0), (diag_ref, diag_out, cols)):
         out[:rows, :cols] = ref[...]
-        out[rows : rows + HALO, :cols] = below_ref[edge : edge + HALO, :]
-        out[rows + HALO :, :cols] = above_ref[edge : edge + HALO, :]
+        out[rows : rows + HALO, :cols] = below[:, edge : edge + cols]
+        out[rows + HALO :, :cols] = above[:, edge : edge + cols]
         sides = []
         for column in (right, left):
             mid = unpack_lanes(got_ref, (g * tiles + column) * width + at, rows)
@@ -232,16 +241,10 @@
     smooth_out[...] = smooth
     left_over = (rhs - (6.0 + diag) * smooth + neighbour_sum(smooth))[:rows, :cols]
     coarse = block_means([left_over])
-    coarse_out[...] = jnp.broadcast_to(coarse, (SUB, LANES))
-
-
-def spread_kernel(keep_ref, came_ref, coarse_ref, slots_ref):
-    high = keep_ref.shape[0]
-    width = high + 1
-    half = keep_ref[...] + came_ref[...]
-    for device in range(slots_ref.shape[0] // width):
-        slots_ref[device * width : device * width + high, :] = half
-        slots_ref[device * width + high : (device + 1) * width, :] = coarse_ref[:1, :]
+    half = half_ref[...]
+    for device in range(groups * tiles):
+        slots_ref[device * (high + 1) : device * (high + 1) + high, :] = half
+        slots_ref[device * (high + 1) + high : (device + 1) * (high + 1), :] = coarse
 
 
 def coarse_operator(value, mean, grid, blocks):
@@ -287,9 +290,10 @@
     )
 
 
-def second_kernel(grid, blocks, got_ref, mean_ref, factor_ref, value_ref, slots_ref):
-    groups, tiles = grid
-    high = factor_ref.shape[1] // LANES // 2
+def second_kernel(grid, blocks, got_ref, mean_ref, mine_ref, value_ref, slots_ref):
+    groups, tiles = grid
+    here = mine_ref.shape[0] - HALO
+    high = mine_ref.shape[1] // LANES // 2
     width = high + 1
     for side in range(2):
         total = None
@@ -300,8 +304,10 @@
         value_ref[side * high : (side + 1) * high, :] = total
     rest = interleave(*pairs(got_ref, high, width))
     coarse = rest - MIX * coarse_operator(value_ref[...], mean_ref[...], grid, blocks)
-    terms = two_products(coarse, factor_ref)
-    for m, term in enumerate(terms):
+    inner = products(coarse, mine_ref, here)
+    for m in range(2 * high):
+        term = mine_ref[:here, m * LANES : (m + 1) * LANES] * inner
+        term = jnp.sum(term, axis=0, keepdims=True)
         slots_ref[2 * m : 2 * m + 1, :] = term
         slots_ref[2 * m + 1 : 2 * m + 2, :] = shift(term, LANES // 2, 1)
 
@@ -374,8 +380,6 @@
     high = points // LANES
     blocks = (rows // FAC, cols // FAC)
     everyone = ("grp", "tile")
-    swap = [(i, i ^ 1) for i in range(groups)]
-    g = lax.axis_index("grp")
 
     def exchange(slots):
         lines = slots.shape[0] // count
@@ -383,58 +387,56 @@
         return got.reshape(count * lines, LANES)
 
     width = 2 * rows * HALO // LANES + 1
-    edge = (2 * HALO, cols)
-    shapes = [(count * width, LANES), (rows, cols), (rows, cols), inverse_factor.shape]
-    shapes += [edge] * (2 if groups > 2 else 1)
-    slots, right_side, diagonal, inverse_factor, *edges = pl.pallas_call(
+    here = inverse_factor.shape[0]
+    shapes = [(count * width, LANES), (rows, cols), (rows, cols), (here + HALO, points)]
+    shapes += [(HALO, 2 * cols)] if groups > 2 else []
+    slots, right_side, diagonal, mine, *edges = pl.pallas_call(
         functools.partial(start_kernel, grid),
         out_shape=[jax.ShapeDtypeStruct(s, jnp.float32) for s in shapes],
         in_specs=[pl.BlockSpec(memory_space=pltpu.HBM)] * 3,
         out_specs=[VMEM] * len(shapes),
         scratch_shapes=[pltpu.SemaphoreType.DMA((3,))],
-        compiler_params=pltpu.CompilerParams(vmem_limit_bytes=LIMIT),
+        compiler_params=pltpu.CompilerParams(vmem_limit_bytes=limit(points)),
     )(
         *[
             pltpu.with_memory_space_constraint(x, pltpu.HBM)
             for x in (right_side, diagonal, inverse_factor)
         ]
     )
-    got = exchange(slots)
-    got, edges = lax.optimization_barrier((got, edges))
-    near = lax.ppermute(edges[0], "grp", swap)
+    theirs = lax.ppermute(mine, "grp", [(i, i ^ 1) for i in range(groups)])
+    far = []
     if groups > 2:
         across = [(i, i + 1) for i in range(1, groups - 1, 2)]
         across += [(j, i) for i, j in across]
-        far = lax.ppermute(edges[1], "grp", across)
-        below = jnp.where(g % 2 == 0, near, far)
-        above = jnp.where(g % 2 == 0, far, near)
-    else:
-        below, above = near, near
-
-    half = (high // 2, LANES)
-    keep, send, mean = call(
-        functools.partial(first_kernel, width), [half, half, (high, LANES)], 2
-    )(got, inverse_factor)
-    came = lax.ppermute(send, "grp", swap)
+        far = [lax.ppermute(edges[0], "grp", across)]
+    got = exchange(slots)
+
     wide = (rows + 2 * HALO, cols + LANES)
-    rhs, diag, weight, smooth, coarse = call(
-        functools.partial(smooth_kernel, grid, width), [wide] * 4 + [(SUB, LANES)], 5
-    )(got, right_side, diagonal, below, above)
-    (slots,) = call(spread_kernel, [(count * (high // 2 + 1), LANES)], 3)(keep, came, coarse)
+    rhs, diag, weight, smooth, mean, slots = call(
+        points,
+        functools.partial(middle_kernel, grid, width),
+        [wide] * 4 + [(high, LANES), (count * (high // 2 + 1), LANES)],
+        5 + len(far),
+        [(high // 2, LANES)],
+    )(got, right_side, diagonal, mine, theirs, *far)
     got = exchange(slots)
 
     value, slots = call(
-        functools.partial(second_kernel, grid, blocks), [(high, LANES), (count, LANES)], 3
-    )(got, mean, inverse_factor)
+        points,
+        functools.partial(second_kernel, grid, blocks),
+        [(high, LANES), (count, LANES)],
+        3,
+    )(got, mean, mine)
     got = exchange(slots)
     (field,) = call(
-        functools.partial(last_kernel, grid), [(rows, cols)], 6, [wide]
+        points, functools.partial(last_kernel, grid), [(rows, cols)], 6, [wide]
     )(got, value, rhs, diag, weight, smooth)
     return field
 
 
 def solution(mesh):
     placed = (P("grp", "tile"), P("grp", "tile"), P(("grp", "tile"), None))
+
     return jax.shard_map(
         shards, mesh=mesh, in_specs=placed, out_specs=P("grp", "tile"), check_vma=False
     )

time: 38.6 us -> 37.5 us (0.972)
  waiting for transfers between devices: 0.42 us -> 0.01 us
  blocking collectives: 33.6 us -> 33.2 us
    ppermute x2 -> x1, waiting for transfers between devices: 0.42 us -> 0.01 us  [shards(): theirs = lax.ppermute(mine, 'grp', [(i, i ^ 1) for i in range(groups)])]
    all_to_all x3, blocking collectives: 33.6 us -> 33.2 us  [exchange(): lax.all_to_all(slots.reshape(count, lines * LANES), everyone, 0, 0, tiled...]
    pallas_call x5 -> x3, Pallas kernels: 2.6 us -> 2.43 us  [the longest x1 1.24 us: shards(): call(points, functools.partial(last_kernel, grid), [(rows, cols)], 6, [wi...]
  transfers between devices with their start and end apart: 2 -> 1, of which waited for: 1 -> 0; matrix products, arithmetic and copies ran while one was open for 0% -> 0% of each run, Pallas kernels for 2% -> 0%
where the time goes in v5:
time: 37.5 us; the launch traced here: 37.4 us
  blocking collectives  33.2 us (89%)
  Pallas kernels  3.57 us (10%)
  starting transfers between devices  0.56 us (1%)
    all_to_all x3, blocking collectives, exchange(): lax.all_to_all(slots.reshape(count, lines * LANES), everyone, 0, 0, tiled...  33.2 us
    pallas_call x1, Pallas kernels, shards(): call(points, functools.partial(last_kernel, grid), [(rows, cols)], 6, [wi...  1.24 us
    pallas_call x1, Pallas kernels, shards(): pl.pallas_call(functools.partial(start_kernel, grid), out_shape=[jax.Shap...  1.14 us
    pallas_call x1, Pallas kernels, shards(): call(points, functools.partial(middle_kernel, grid, width), [wide] * 4 +...  0.8 us
  transfers between devices with their start and end apart: 1, of which 0 were waited for; matrix products, arithmetic and copies ran while one was open for 0% of the time, Pallas kernels for 0%

profile of v5, /device:TPU:0, one launch (start us, length us, event | category | flops | bytes accessed | tf_op | source)
XLA Modules:
  0.0 37.4 jit_solution(13485449555294226856)
XLA Ops:
  0.0 1.1 %shard_map.37 = (f32[160,128]{1,0:T(8,128)S(1)}, f32[32,512]{1,0:T(8,128)S(1)}, f32[32,512]{1,0:T(8,128)S(1)}, f32[72,2048]{1,0:T(8,128)S(1)}) custom-call(f32[32,512]{1,0:T(8,128)} %rhs_in.1, f32[32,512]{1,0:T(8,128)} %diag_in.1, f32[64,2048]{1,0:T(8,128)} %factor_in.1), custom_call_target="tpu_custom_call" | custom-call | tf_op jit(solution)/shard_map/pallas_call | solution.py:393
  1.2 0.6 %collective-permute-start = (f32[72,2048]{1,0:T(8,128)S(1)}, f32[72,2048]{1,0:T(8,128)S(1)}, u32[]{:S(2)}, u32[]{:S(2)}) collective-permute-start(f32[72,2048]{1,0:T(8,128)S(1)} %get-tuple-element.20.mine_ref), channel_id=1, source_target_pairs={{0,16},{16,0},{1,17},{17,1},{2,18},{18,2},{3,19},{19,3},{4,20},{20... | collective-permute-start | bytes 1769480 | tf_op jit(solution)/shard_map/ppermute | solution.py:406
  1.7 14.2 %all_to_all.29 = f32[32,1,640]{2,1,0:T(1,128)S(1)} all-to-all(f32[32,1,640]{2,1,0:T(1,128)S(1)} %bitcast.11), channel_id=1, replica_groups=mesh['grp'=2,'tile'=16] {'grp','tile'}, dimensions={0} | all-to-all | bytes 163840 | tf_op jit(solution)/shard_map/all_to_all | solution.py:386
  15.9 0.0 collective-permute-done.theirs_ref
  15.9 0.8 %shard_map.38 = (f32[48,640]{1,0:T(8,128)S(1)}, f32[48,640]{1,0:T(8,128)S(1)}, f32[48,640]{1,0:T(8,128)S(1)}, f32[48,640]{1,0:T(8,128)S(1)}, f32[16,128]{1,0:T(8,128)S(1)}, /*index=5*/f32[288,128]{1,0:T(8,128)S(1)}) custom-call(f32[160,128]{1,0:T(8,128)S(1)} %bitcast.9, f32[32,512]{1,0:T(8,128)S(1)} %get-tuple-element.18.rhs_ref, ...), custom_call_target="tpu_custom_call" | custom-call | tf_op jit(solution)/shard_map/pallas_call | solution.py:415
  16.7 9.9 %all_to_all.30 = f32[32,1,1152]{2,1,0:T(1,128)S(1)} all-to-all(f32[32,1,1152]{2,1,0:T(1,128)S(1)} %bitcast.10), channel_id=1, replica_groups=mesh['grp'=2,'tile'=16] {'grp','tile'}, dimensions={0} | all-to-all | bytes 294912 | tf_op jit(solution)/shard_map/all_to_all | solution.py:386
  26.7 0.4 %shard_map.39 = (f32[16,128]{1,0:T(8,128)S(1)}, f32[32,128]{1,0:T(8,128)S(1)}) custom-call(f32[288,128]{1,0:T(8,128)S(1)} %bitcast.8, f32[16,128]{1,0:T(8,128)S(1)} %get-tuple-element.22.mean_ref, f32[72,2048]{1,0:T(8,128)S(1)} %get-tuple-element.20.mine_ref), custom_call_target="tpu_custom_call" | custom-call | tf_op jit(solution)/shard_map/pallas_call | solution.py:424
  27.0 9.1 %all_to_all.31 = f32[32,1,128]{2,1,0:T(1,128)S(1)} all-to-all(f32[32,1,128]{2,1,0:T(1,128)S(1)} %bitcast.13), channel_id=1, replica_groups=mesh['grp'=2,'tile'=16] {'grp','tile'}, dimensions={0} | all-to-all | bytes 32768 | tf_op jit(solution)/shard_map/all_to_all | solution.py:386
  36.1 1.2 %shard_map.40 = f32[32,512]{1,0:T(8,128)} custom-call(f32[32,128]{1,0:T(8,128)S(1)} %bitcast.12, f32[16,128]{1,0:T(8,128)S(1)} %get-tuple-element.24.value_ref, f32[48,640]{1,0:T(8,128)S(1)} %get-tuple-element.25.rhs_ref, f32[48,640]{1,0:T(8,128)S(1)} %get-tuple-element.26.diag_ref, f32[48,640]{1,0:T(8,128)S(1)} %get-tuple-element.27.weight_ref, ...), custom_call_target="tpu_custom_call" | custom-call | tf_op jit(solution)/shard_map/pallas_call | solution.py:431
Async XLA Ops:
  1.2 14.8 %collective-permute-start = (f32[72,2048]{1,0:T(8,128)S(1)}, f32[72,2048]{1,0:T(8,128)S(1)}, u32[]{:S(2)}, u32[]{:S(2)}) collective-permute-start(f32[72,2048]{1,0:T(8,128)S(1)} %get-tuple-element.20.mine_ref), channel_id=1, source_target_pairs={{0,16},{16,0},{1,17},{17,1},{2,18},{18,2},{3,19},{19,3},{4,20},{20... | collective-permute-start | bytes 1769480 | tf_op jit(solution)/shard_map/ppermute | solution.py:406

commit v6 on v5

--- a/solution.py
+++ b/solution.py
@@ -184,25 +184,32 @@
 def middle_kernel(
     grid, width, got_ref, rhs_ref, diag_ref, mine_ref, theirs_ref, *refs
 ):
-    far_refs, (rhs_out, diag_out, weight_out, smooth_out, mean_ref, slots_ref, half_ref) = (
-        refs[:-7],
-        refs[-7:],
-    )
+    far_refs, outs = refs[:-8], refs[-8:]
+    rhs_out, diag_out, weight_out, smooth_out, term_ref, ring_ref, slots_ref, term_scr = outs
     groups, tiles = grid
     g, t = lax.axis_index("grp"), lax.axis_index("tile")
     rows, cols = rhs_ref.shape
     here = mine_ref.shape[0] - HALO
-    high = half_ref.shape[0]
     even, odd = pairs(got_ref, width - 1, width)
-    mean_ref[...] = interleave(shift(even, LANES // 2, 1), odd)
+    mean = interleave(shift(even, LANES // 2, 1), odd)
     vector = interleave(even, shift(odd, LANES // 2, 1))
     inner = products(vector, mine_ref, here)
     other = products(vector, theirs_ref, here)
-    start = lax.rem(g, 2) * (high * LANES)
-    for m in range(high):
-        place = pl.ds(pl.multiple_of(start + m * LANES, LANES), LANES)
+    for m in range(vector.shape[0]):
+        place = slice(m * LANES, (m + 1) * LANES)
         term = mine_ref[:here, place] * inner + theirs_ref[:here, place] * other
-        half_ref[m : m + 1, :] = jnp.sum(term, axis=0, keepdims=True)
+        term_scr[m : m + 1, :] = jnp.sum(term, axis=0, keepdims=True)
+    term = term_scr[...]
+    coarse_grid = Coarse(term.shape, grid, (rows // FAC, cols // FAC))
+    next_rhs = -MIX * coarse_operator(term, mean, coarse_grid)
+    own = lax.rem(coarse_grid.group, 2) == lax.rem(g, 2)
+    ends, columns = (jnp.where(own, x, 0.0) for x in around(term, coarse_grid))
+    term = jnp.where(own, term, 0.0)
+    half_lane = LANES // 2
+    for k, x in enumerate((shift(term, half_lane, 1), term)):
+        term_ref[k] = x
+    ring_ref[0] = interleave(ends, shift(columns, half_lane, 1))
+    ring_ref[1] = interleave(shift(ends, half_lane, 1), columns)
     near_ref = theirs_ref.at[here:, :]
     if groups > 2:
         near, far = near_ref[:, : 2 * cols], far_refs[0][...]
@@ -241,75 +248,104 @@
     smooth_out[...] = smooth
     left_over = (rhs - (6.0 + diag) * smooth + neighbour_sum(smooth))[:rows, :cols]
     coarse = block_means([left_over])
-    half = half_ref[...]
+    per_group = coarse_grid.per_group
+    is_even = lax.rem(g, 2) == 0
+    half = jnp.concatenate(
+        [
+            jnp.where(is_even, next_rhs[k : k + per_group], next_rhs[k + per_group : k + 2 * per_group])
+            for k in range(0, groups * per_group, 2 * per_group)
+        ],
+        axis=0,
+    )
+    at = (g // 2) * tiles + t
+    devices = LANES // here
+    mine = row_iota(half.shape) * devices + lane_iota(half.shape) // here == at
+    half = half + jnp.where(mine, coarse, 0.0)
+    high = half.shape[0]
     for device in range(groups * tiles):
-        slots_ref[device * (high + 1) : device * (high + 1) + high, :] = half
-        slots_ref[device * (high + 1) + high : (device + 1) * (high + 1), :] = coarse
-
-
-def coarse_operator(value, mean, grid, blocks):
-    groups, tiles = grid
-    block_rows, per_row = blocks
-    here = block_rows * per_row
-    shape = value.shape
-    lane, row = lane_iota(shape), row_iota(shape)
-    device = row * (LANES // here) + lane // here
-    a = lax.rem(lane, here) // per_row
-    b = lax.rem(lane, per_row)
-    tile, group = lax.rem(device, tiles), device // tiles
-    per_line = tiles * here // LANES
-
-    def to_right(x):
+        slots_ref[device * high : (device + 1) * high, :] = half
+
+
+class Coarse:
+    def __init__(self, shape, grid, blocks):
+        self.groups, self.tiles = grid
+        self.block_rows, self.per_row = blocks
+        self.here = self.block_rows * self.per_row
+        self.per_group = self.tiles * self.here // LANES
+        self.lane = lane_iota(shape)
+        device = row_iota(shape) * (LANES // self.here) + self.lane // self.here
+        self.a = lax.rem(self.lane, self.here) // self.per_row
+        self.b = lax.rem(self.lane, self.per_row)
+        self.tile, self.group = lax.rem(device, self.tiles), device // self.tiles
+
+    def left_of(self, x):
         near = shift(x, 1, 1)
-        far = shift(x, here - per_row + 1, 1)
-        far = jnp.where(lane < here, shift(far, 1, 0), far)
-        return jnp.where(b > 0, near, jnp.where(tile > 0, far, 0.0))
-
-    def to_left(x):
+        far = shift(x, self.here - self.per_row + 1, 1)
+        far = jnp.where(self.lane < self.here, shift(far, 1, 0), far)
+        return jnp.where(self.b > 0, near, jnp.where(self.tile > 0, far, 0.0))
+
+    def right_of(self, x):
         near = shift(x, -1, 1)
-        far = shift(x, -(here - per_row + 1), 1)
-        far = jnp.where(lane >= LANES - here, shift(far, -1, 0), far)
-        return jnp.where(b < per_row - 1, near, jnp.where(tile < tiles - 1, far, 0.0))
-
-    def to_below(x):
-        near = shift(x, per_row, 1)
-        far = shift(shift(x, -(here - per_row), 1), per_line, 0)
-        return jnp.where(a > 0, near, jnp.where(group > 0, far, 0.0))
-
-    def to_above(x):
-        near = shift(x, -per_row, 1)
-        far = shift(shift(x, here - per_row, 1), -per_line, 0)
-        return jnp.where(a < block_rows - 1, near, jnp.where(group < groups - 1, far, 0.0))
-
-    above, below = to_below(value), to_above(value)
-    sides = above + below + to_right(value) + to_left(value)
-    corners = to_left(above) + to_right(below)
+        far = shift(x, -(self.here - self.per_row + 1), 1)
+        far = jnp.where(self.lane >= LANES - self.here, shift(far, -1, 0), far)
+        last = self.tile < self.tiles - 1
+        return jnp.where(self.b < self.per_row - 1, near, jnp.where(last, far, 0.0))
+
+    def above(self, x):
+        near = shift(x, self.per_row, 1)
+        far = shift(shift(x, -(self.here - self.per_row), 1), self.per_group, 0)
+        return jnp.where(self.a > 0, near, jnp.where(self.group > 0, far, 0.0))
+
+    def below(self, x):
+        near = shift(x, -self.per_row, 1)
+        far = shift(shift(x, self.here - self.per_row, 1), -self.per_group, 0)
+        last = self.group < self.groups - 1
+        return jnp.where(self.a < self.block_rows - 1, near, jnp.where(last, far, 0.0))
+
+
+def coarse_operator(x, mean, coarse):
+    above, below = coarse.above(x), coarse.below(x)
+    sides = above + below + coarse.left_of(x) + coarse.right_of(x)
+    corners = coarse.right_of(above) + coarse.left_of(below)
     edge = 2.0 * FAC - 1.0
-    return mean * value + (edge * (4.0 * value - sides) + (2.0 * value - corners)) * (
-        1.0 / (FAC * FAC)
-    )
-
-
-def second_kernel(grid, blocks, got_ref, mean_ref, mine_ref, value_ref, slots_ref):
+    return mean * x + (edge * (4.0 * x - sides) + (2.0 * x - corners)) * (1.0 / (FAC * FAC))
+
+
+def around(x, coarse):
+    ends = jnp.where(coarse.a == 0, coarse.above(x), coarse.below(x))
+    last = coarse.per_row - 1
+
+    def sides(y):
+        return jnp.where(coarse.b == 0, coarse.left_of(y), coarse.right_of(y))
+
+    own, outer = sides(x), sides(ends)
+    columns = jnp.where(coarse.b == 1, shift(outer, 1, 1), own)
+    return ends, jnp.where(coarse.b == last - 1, shift(outer, -1, 1), columns)
+
+
+def second_kernel(grid, per_group, got_ref, mine_ref, term_ref, ring_ref, slots_ref, value_ref):
     groups, tiles = grid
     here = mine_ref.shape[0] - HALO
-    high = mine_ref.shape[1] // LANES // 2
-    width = high + 1
+    lines = mine_ref.shape[1] // LANES
+    high = lines // 2
+    parts = [None] * groups
     for side in range(2):
         total = None
         for g in range(side, groups, 2):
             for device in range(g * tiles, (g + 1) * tiles):
-                part = got_ref[device * width : device * width + high, :]
+                part = got_ref[device * high : (device + 1) * high, :]
                 total = part if total is None else total + part
-        value_ref[side * high : (side + 1) * high, :] = total
-    rest = interleave(*pairs(got_ref, high, width))
-    coarse = rest - MIX * coarse_operator(value_ref[...], mean_ref[...], grid, blocks)
-    inner = products(coarse, mine_ref, here)
-    for m in range(2 * high):
+        for k in range(groups // 2):
+            parts[2 * k + side] = total[k * per_group : (k + 1) * per_group]
+    inner = products(jnp.concatenate(parts, axis=0), mine_ref, here)
+    for m in range(lines):
         term = mine_ref[:here, m * LANES : (m + 1) * LANES] * inner
-        term = jnp.sum(term, axis=0, keepdims=True)
-        slots_ref[2 * m : 2 * m + 1, :] = term
-        slots_ref[2 * m + 1 : 2 * m + 2, :] = shift(term, LANES // 2, 1)
+        value_ref[m : m + 1, :] = jnp.sum(term, axis=0, keepdims=True)
+    value = value_ref[...]
+    slots_ref[pl.ds(0, lines, stride=4), :] = interleave(value, term_ref[0])
+    slots_ref[pl.ds(1, lines, stride=4), :] = ring_ref[0]
+    slots_ref[pl.ds(2, lines, stride=4), :] = interleave(shift(value, LANES // 2, 1), term_ref[1])
+    slots_ref[pl.ds(3, lines, stride=4), :] = ring_ref[1]
 
 
 def prolong_line(line, first, shape):
@@ -317,39 +353,28 @@
     return gather_lanes(jnp.broadcast_to(line, shape), index)
 
 
-def last_kernel(
-    grid, got_ref, value_ref, rhs_ref, diag_ref, weight_ref, smooth_ref, out_ref, field_ref
-):
-    groups, tiles = grid
-    g, t = lax.axis_index("grp"), lax.axis_index("tile")
+def last_kernel(grid, got_ref, rhs_ref, diag_ref, weight_ref, smooth_ref, out_ref, field_ref):
     rows, cols = out_ref.shape
-    block_rows, per_row = rows // FAC, cols // FAC
+    block_rows, per_row, per_tile = rows // FAC, cols // FAC, LANES // FAC
     here = block_rows * per_row
     inside = inside_mask(grid, rows, cols)
-    up, down = jnp.maximum(g - 1, 0), jnp.minimum(g + 1, groups - 1)
-    left, right = jnp.maximum(t - 1, 0), jnp.minimum(t + 1, tiles - 1)
-
-    def line_of(device):
-        return value_ref[pl.ds(device * here // LANES, 1), :], lax.rem(device * here, LANES)
-
-    bands = [(a * FAC, FAC, g, a) for a in range(block_rows)]
-    bands += [(rows, HALO, down, 0), (rows + HALO, HALO, up, block_rows - 1)]
-    for start, height, group, a in bands:
-        shape = (SUB, LANES)
-        line, at = line_of(group * tiles + t)
-        parts = [
-            prolong_line(line, at + a * per_row + q * (LANES // FAC), shape)
-            for q in range(cols // LANES)
-        ]
-        line, at = line_of(group * tiles + right)
-        beside = gather_lanes(
-            jnp.broadcast_to(line, shape), jnp.full(shape, at + a * per_row, jnp.int32)
-        )
-        line, at = line_of(group * tiles + left)
-        other = gather_lanes(
-            jnp.broadcast_to(line, shape),
-            jnp.full(shape, at + (a + 1) * per_row - 1, jnp.int32),
-        )
+    shape = (SUB, LANES)
+    total = got_ref[:SUB, :]
+    for at in range(SUB, got_ref.shape[0], SUB):
+        total = total + got_ref[at : at + SUB, :]
+    total = total + shift(total, SUB // 2, 0)
+    total = total + shift(total, SUB // 4, 0)
+    second, ring = total[:1], total[1:2]
+
+    def pick(line, at):
+        return gather_lanes(jnp.broadcast_to(line, shape), jnp.full(shape, at, jnp.int32))
+
+    bands = [(a * FAC, FAC, second, here + a * per_row, here + a * per_row) for a in range(block_rows)]
+    bands += [(rows, HALO, ring, per_row, here + per_row), (rows + HALO, HALO, ring, 0, here)]
+    for start, height, line, at, side in bands:
+        parts = [prolong_line(line, at + q * per_tile, shape) for q in range(cols // LANES)]
+        step = 0 if start < rows else 1
+        beside, other = pick(ring, side + per_row - 1 - step), pick(ring, side + step)
         parts.append(jnp.where(lane_iota(shape) < LANES // 2, beside, other))
         for low in range(start, start + height, SUB):
             for q, part in enumerate(parts):
@@ -362,7 +387,7 @@
     for _ in range(SWEEPS - 1):
         smooth = (1.0 - OMEGA) * smooth + weight * (rest + neighbour_sum(smooth))
     base = field[:rows, :cols] + smooth[:rows, :cols]
-    line = MIX * jnp.sum(got_ref[...], axis=0, keepdims=True)
+    line = MIX * second
     for a in range(rows // FAC):
         for q in range(cols // LANES):
             part = prolong_line(line, a * per_row + q * (LANES // FAC), (SUB, LANES))
@@ -378,7 +403,7 @@
     rows, cols = right_side.shape
     points = inverse_factor.shape[1]
     high = points // LANES
-    blocks = (rows // FAC, cols // FAC)
+    assert 2 * inverse_factor.shape[0] == LANES and rows == 2 * FAC and groups % 2 == 0
     everyone = ("grp", "tile")
 
     def exchange(slots):
@@ -412,31 +437,30 @@
     got = exchange(slots)
 
     wide = (rows + 2 * HALO, cols + LANES)
-    rhs, diag, weight, smooth, mean, slots = call(
+    rhs, diag, weight, smooth, term, ring, slots = call(
         points,
         functools.partial(middle_kernel, grid, width),
-        [wide] * 4 + [(high, LANES), (count * (high // 2 + 1), LANES)],
+        [wide] * 4 + [(2, high, LANES)] * 2 + [(count * high // 2, LANES)],
         5 + len(far),
-        [(high // 2, LANES)],
+        [(high, LANES)],
     )(got, right_side, diagonal, mine, theirs, *far)
     got = exchange(slots)
 
-    value, slots = call(
+    (slots,) = call(
         points,
-        functools.partial(second_kernel, grid, blocks),
-        [(high, LANES), (count, LANES)],
-        3,
-    )(got, mean, mine)
+        functools.partial(second_kernel, grid, high // groups),
+        [(2 * count, LANES)],
+        4,
+        [(high, LANES)],
+    )(got, mine, term, ring)
     got = exchange(slots)
     (field,) = call(
-        points, functools.partial(last_kernel, grid), [(rows, cols)], 6, [wide]
-    )(got, value, rhs, diag, weight, smooth)
+        points, functools.partial(last_kernel, grid), [(rows, cols)], 5, [wide]
+    )(got, rhs, diag, weight, smooth)
     return field
 
 
 def solution(mesh):
     placed = (P("grp", "tile"), P("grp", "tile"), P(("grp", "tile"), None))
 
-    return jax.shard_map(
-        shards, mesh=mesh, in_specs=placed, out_specs=P("grp", "tile"), check_vma=False
-    )
+    return jax.shard_map(shards, mesh=mesh, in_specs=placed, out_specs=P("grp", "tile"), check_vma=False)

time: 37.5 us -> 37.2 us (level)
  no operation moved by 1% of the time
where the time goes in v6:
time: 37.2 us; the launch traced here: 37 us
  blocking collectives  32.9 us (88%)
  Pallas kernels  3.56 us (10%)
  starting transfers between devices  0.56 us (2%)
    all_to_all x3, blocking collectives, exchange(): lax.all_to_all(slots.reshape(count, lines * LANES), everyone, 0, 0, tiled...  32.9 us
    pallas_call x1, Pallas kernels, shards(): call(points, functools.partial(last_kernel, grid), [(rows, cols)], 5, [wi...  1.27 us
    pallas_call x1, Pallas kernels, shards(): pl.pallas_call(functools.partial(start_kernel, grid), out_shape=[jax.Shap...  1.14 us
    pallas_call x1, Pallas kernels, shards(): call(points, functools.partial(middle_kernel, grid, width), [wide] * 4 +...  0.9 us
  transfers between devices with their start and end apart: 1, of which 0 were waited for; matrix products, arithmetic and copies ran while one was open for 0% of the time, Pallas kernels for 0%

profile of v6, /device:TPU:0, one launch (start us, length us, event | category | flops | bytes accessed | tf_op | source)
XLA Modules:
  0.0 37.0 jit_solution(13131194226796691514)
XLA Ops:
  0.0 1.1 %shard_map.37 = (f32[160,128]{1,0:T(8,128)S(1)}, f32[32,512]{1,0:T(8,128)S(1)}, f32[32,512]{1,0:T(8,128)S(1)}, f32[72,2048]{1,0:T(8,128)S(1)}) custom-call(f32[32,512]{1,0:T(8,128)} %rhs_in.1, f32[32,512]{1,0:T(8,128)} %diag_in.1, f32[64,2048]{1,0:T(8,128)} %factor_in.1), custom_call_target="tpu_custom_call" | custom-call | tf_op jit(solution)/shard_map/pallas_call | solution.py:418
  1.2 0.6 %collective-permute-start = (f32[72,2048]{1,0:T(8,128)S(1)}, f32[72,2048]{1,0:T(8,128)S(1)}, u32[]{:S(2)}, u32[]{:S(2)}) collective-permute-start(f32[72,2048]{1,0:T(8,128)S(1)} %get-tuple-element.19.mine_ref), channel_id=1, source_target_pairs={{0,16},{16,0},{1,17},{17,1},{2,18},{18,2},{3,19},{19,3},{4,20},{20... | collective-permute-start | bytes 1769480 | tf_op jit(solution)/shard_map/ppermute | solution.py:431
  1.7 14.2 %all_to_all.27 = f32[32,1,640]{2,1,0:T(1,128)S(1)} all-to-all(f32[32,1,640]{2,1,0:T(1,128)S(1)} %bitcast.11), channel_id=1, replica_groups=mesh['grp'=2,'tile'=16] {'grp','tile'}, dimensions={0} | all-to-all | bytes 163840 | tf_op jit(solution)/shard_map/all_to_all | solution.py:411
  15.9 0.0 collective-permute-done.theirs_ref
  15.9 0.9 %shard_map.38 = (f32[48,640]{1,0:T(8,128)S(1)}, f32[48,640]{1,0:T(8,128)S(1)}, f32[48,640]{1,0:T(8,128)S(1)}, f32[48,640]{1,0:T(8,128)S(1)}, f32[2,16,128]{2,1,0...) custom-call(f32[160,128]{1,0:T(8,128)S(1)} %bitcast.7, f32[32,512]{1,0:T(8,128)S(1)} %get-tuple-element.17.rhs_ref, ...), custom_call_target="tpu_custom_call" | custom-call | tf_op jit(solution)/shard_map/pallas_call | solution.py:440
  16.8 9.7 %all_to_all.28 = f32[32,1,1024]{2,1,0:T(1,128)S(1)} all-to-all(f32[32,1,1024]{2,1,0:T(1,128)S(1)} %bitcast.10), channel_id=1, replica_groups=mesh['grp'=2,'tile'=16] {'grp','tile'}, dimensions={0} | all-to-all | bytes 262144 | tf_op jit(solution)/shard_map/all_to_all | solution.py:411
  26.5 0.2 shard_map.39
  26.7 9.0 %all_to_all.29 = f32[32,1,256]{2,1,0:T(1,128)S(1)} all-to-all(f32[32,1,256]{2,1,0:T(1,128)S(1)} %bitcast.9), channel_id=1, replica_groups=mesh['grp'=2,'tile'=16] {'grp','tile'}, dimensions={0} | all-to-all | bytes 65536 | tf_op jit(solution)/shard_map/all_to_all | solution.py:411
  35.8 1.3 %shard_map.40 = f32[32,512]{1,0:T(8,128)} custom-call(f32[64,128]{1,0:T(8,128)S(1)} %bitcast.8, f32[48,640]{1,0:T(8,128)S(1)} %get-tuple-element.23.rhs_ref, f32[48,640]{1,0:T(8,128)S(1)} %get-tuple-element.24.diag_ref, f32[48,640]{1,0:T(8,128)S(1)} %get-tuple-element.25.weight_ref, f32[48,640]{1,0:T(8,128)S(1)} %get-tuple-element.26.smooth_ref), custom_call_target="tpu_custom_call" | custom-call | tf_op jit(solution)/shard_map/pallas_call | solution.py:457
Async XLA Ops:
  1.2 14.8 %collective-permute-start = (f32[72,2048]{1,0:T(8,128)S(1)}, f32[72,2048]{1,0:T(8,128)S(1)}, u32[]{:S(2)}, u32[]{:S(2)}) collective-permute-start(f32[72,2048]{1,0:T(8,128)S(1)} %get-tuple-element.19.mine_ref), channel_id=1, source_target_pairs={{0,16},{16,0},{1,17},{17,1},{2,18},{18,2},{3,19},{19,3},{4,20},{20... | collective-permute-start | bytes 1769480 | tf_op jit(solution)/shard_map/ppermute | solution.py:431

commit v7 on v6

--- a/solution.py
+++ b/solution.py
@@ -137,10 +137,10 @@
     loads[2].wait()
 
 
-def products(vector, factor_ref, here):
+def products(vector, factor_ref, here, first_lane=lambda m: m * LANES):
     total = None
     for m in range(vector.shape[0]):
-        term = factor_ref[:here, m * LANES : (m + 1) * LANES] * vector[m : m + 1, :]
+        term = factor_ref[:here, pl.ds(first_lane(m), LANES)] * vector[m : m + 1, :]
         total = term if total is None else total + term
     return jnp.sum(total, axis=1, keepdims=True)
 
@@ -249,21 +249,27 @@
     left_over = (rhs - (6.0 + diag) * smooth + neighbour_sum(smooth))[:rows, :cols]
     coarse = block_means([left_over])
     per_group = coarse_grid.per_group
-    is_even = lax.rem(g, 2) == 0
-    half = jnp.concatenate(
-        [
-            jnp.where(is_even, next_rhs[k : k + per_group], next_rhs[k + per_group : k + 2 * per_group])
-            for k in range(0, groups * per_group, 2 * per_group)
-        ],
-        axis=0,
-    )
     at = (g // 2) * tiles + t
     devices = LANES // here
-    mine = row_iota(half.shape) * devices + lane_iota(half.shape) // here == at
-    half = half + jnp.where(mine, coarse, 0.0)
-    high = half.shape[0]
-    for device in range(groups * tiles):
-        slots_ref[device * high : (device + 1) * high, :] = half
+    parity = lax.rem(g, 2)
+    high = groups // 2 * per_group
+    part = high // 2
+    for k in range(2):
+        half = jnp.concatenate(
+            [
+                next_rhs[m : m + per_group]
+                for m in range(k * per_group, groups * per_group, 2 * per_group)
+            ],
+            axis=0,
+        )
+        place = row_iota(half.shape) * devices + lane_iota(half.shape) // here
+        half = half + jnp.where((place == at) & (parity == k), coarse, 0.0)
+        is_first = lax.rem(at * here // LANES // part + parity + k, 2) == 0
+        sent = jnp.where(is_first, half[:part], half[part:])
+        sent = jnp.concatenate([sent, sent], axis=0)
+        for group in range(k, groups, 2):
+            for device in range(group * tiles, (group + 1) * tiles, 2):
+                slots_ref[device * part : (device + 2) * part, :] = sent
 
 
 class Coarse:
@@ -323,23 +329,35 @@
     return ends, jnp.where(coarse.b == last - 1, shift(outer, -1, 1), columns)
 
 
-def second_kernel(grid, per_group, got_ref, mine_ref, term_ref, ring_ref, slots_ref, value_ref):
+def second_kernel(
+    grid, per_group, got_ref, mine_ref, theirs_ref, term_ref, ring_ref, slots_ref, value_ref
+):
     groups, tiles = grid
+    parity = lax.rem(lax.axis_index("grp"), 2)
     here = mine_ref.shape[0] - HALO
     lines = mine_ref.shape[1] // LANES
-    high = lines // 2
-    parts = [None] * groups
-    for side in range(2):
-        total = None
-        for g in range(side, groups, 2):
-            for device in range(g * tiles, (g + 1) * tiles):
-                part = got_ref[device * high : (device + 1) * high, :]
-                total = part if total is None else total + part
-        for k in range(groups // 2):
-            parts[2 * k + side] = total[k * per_group : (k + 1) * per_group]
-    inner = products(jnp.concatenate(parts, axis=0), mine_ref, here)
+    part = lines // 4
+    sums = [None, None]
+    for device in range(0, groups * tiles, 2):
+        group, tile = device // tiles, device % tiles
+        line = (group // 2 * tiles + tile) * here // LANES
+        k = (line // part + group) % 2
+        got = got_ref[device * part : (device + 2) * part, :]
+        sums[k] = got if sums[k] is None else sums[k] + got
+    one, two = [x[:part] + x[part:] for x in sums]
+    coarse = jnp.concatenate(
+        [jnp.where(parity == 0, one, two), jnp.where(parity == 0, two, one)], axis=0
+    )
+
+    def first_lane(m):
+        line = (m // per_group * 2 + parity) * per_group + m % per_group
+        return pl.multiple_of(line * LANES, LANES)
+
+    inner = products(coarse, mine_ref, here, first_lane)
+    other = products(coarse, theirs_ref, here, first_lane)
     for m in range(lines):
-        term = mine_ref[:here, m * LANES : (m + 1) * LANES] * inner
+        place = slice(m * LANES, (m + 1) * LANES)
+        term = mine_ref[:here, place] * inner + theirs_ref[:here, place] * other
         value_ref[m : m + 1, :] = jnp.sum(term, axis=0, keepdims=True)
     value = value_ref[...]
     slots_ref[pl.ds(0, lines, stride=4), :] = interleave(value, term_ref[0])
@@ -440,7 +458,7 @@
     rhs, diag, weight, smooth, term, ring, slots = call(
         points,
         functools.partial(middle_kernel, grid, width),
-        [wide] * 4 + [(2, high, LANES)] * 2 + [(count * high // 2, LANES)],
+        [wide] * 4 + [(2, high, LANES)] * 2 + [(count * high // 4, LANES)],
         5 + len(far),
         [(high, LANES)],
     )(got, right_side, diagonal, mine, theirs, *far)
@@ -450,9 +468,9 @@
         points,
         functools.partial(second_kernel, grid, high // groups),
         [(2 * count, LANES)],
-        4,
+        5,
         [(high, LANES)],
-    )(got, mine, term, ring)
+    )(got, mine, theirs, term, ring)
     got = exchange(slots)
     (field,) = call(
         points, functools.partial(last_kernel, grid), [(rows, cols)], 5, [wide]
@@ -463,4 +481,6 @@
 def solution(mesh):
     placed = (P("grp", "tile"), P("grp", "tile"), P(("grp", "tile"), None))
 
-    return jax.shard_map(shards, mesh=mesh, in_specs=placed, out_specs=P("grp", "tile"), check_vma=False)
+    return jax.shard_map(
+        shards, mesh=mesh, in_specs=placed, out_specs=P("grp", "tile"), check_vma=False
+    )

time: 37.2 us -> 36.5 us (0.981)
  blocking collectives: 32.9 us -> 32.1 us
    all_to_all x3, blocking collectives: 32.9 us -> 32.1 us  [exchange(): lax.all_to_all(slots.reshape(count, lines * LANES), everyone, 0, 0, tiled...]
where the time goes in v7:
time: 36.5 us; the launch traced here: 36.3 us
  blocking collectives  32.1 us (88%)
  Pallas kernels  3.62 us (10%)
  starting transfers between devices  0.56 us (2%)
    all_to_all x3, blocking collectives, exchange(): lax.all_to_all(slots.reshape(count, lines * LANES), everyone, 0, 0, tiled...  32.1 us
    pallas_call x1, Pallas kernels, shards(): call(points, functools.partial(last_kernel, grid), [(rows, cols)], 5, [wi...  1.27 us
    pallas_call x1, Pallas kernels, shards(): pl.pallas_call(functools.partial(start_kernel, grid), out_shape=[jax.Shap...  1.14 us
    pallas_call x1, Pallas kernels, shards(): call(points, functools.partial(middle_kernel, grid, width), [wide] * 4 +...  0.91 us
  transfers between devices with their start and end apart: 1, of which 0 were waited for; matrix products, arithmetic and copies ran while one was open for 0% of the time, Pallas kernels for 0%

profile of v7, /device:TPU:0, one launch (start us, length us, event | category | flops | bytes accessed | tf_op | source)
XLA Modules:
  0.0 36.3 jit_solution(12028542478544566658)
XLA Ops:
  0.0 1.1 %shard_map.37 = (f32[160,128]{1,0:T(8,128)S(1)}, f32[32,512]{1,0:T(8,128)S(1)}, f32[32,512]{1,0:T(8,128)S(1)}, f32[72,2048]{1,0:T(8,128)S(1)}) custom-call(f32[32,512]{1,0:T(8,128)} %rhs_in.1, f32[32,512]{1,0:T(8,128)} %diag_in.1, f32[64,2048]{1,0:T(8,128)} %factor_in.1), custom_call_target="tpu_custom_call" | custom-call | tf_op jit(solution)/shard_map/pallas_call | solution.py:436
  1.2 0.6 %collective-permute-start = (f32[72,2048]{1,0:T(8,128)S(1)}, f32[72,2048]{1,0:T(8,128)S(1)}, u32[]{:S(2)}, u32[]{:S(2)}) collective-permute-start(f32[72,2048]{1,0:T(8,128)S(1)} %get-tuple-element.19.mine_ref), channel_id=1, source_target_pairs={{0,16},{16,0},{1,17},{17,1},{2,18},{18,2},{3,19},{19,3},{4,20},{20... | collective-permute-start | bytes 1769480 | tf_op jit(solution)/shard_map/ppermute | solution.py:449
  1.7 14.2 %all_to_all.27 = f32[32,1,640]{2,1,0:T(1,128)S(1)} all-to-all(f32[32,1,640]{2,1,0:T(1,128)S(1)} %bitcast.10), channel_id=1, replica_groups=mesh['grp'=2,'tile'=16] {'grp','tile'}, dimensions={0} | all-to-all | bytes 163840 | tf_op jit(solution)/shard_map/all_to_all | solution.py:429
  15.9 0.0 collective-permute-done.theirs_ref
  15.9 0.9 %shard_map.38 = (f32[48,640]{1,0:T(8,128)S(1)}, f32[48,640]{1,0:T(8,128)S(1)}, f32[48,640]{1,0:T(8,128)S(1)}, f32[48,640]{1,0:T(8,128)S(1)}, f32[2,16,128]{2,1,0...) custom-call(f32[160,128]{1,0:T(8,128)S(1)} %bitcast.6, f32[32,512]{1,0:T(8,128)S(1)} %get-tuple-element.17.rhs_ref, ...), custom_call_target="tpu_custom_call" | custom-call | tf_op jit(solution)/shard_map/pallas_call | solution.py:458
  16.8 9.0 %all_to_all.28 = f32[32,1,512]{2,1,0:T(1,128)S(1)} all-to-all(f32[32,1,512]{2,1,0:T(1,128)S(1)} %bitcast.11), channel_id=1, replica_groups=mesh['grp'=2,'tile'=16] {'grp','tile'}, dimensions={0} | all-to-all | bytes 131072 | tf_op jit(solution)/shard_map/all_to_all | solution.py:429
  25.8 0.3 shard_map.39
  26.1 8.9 %all_to_all.29 = f32[32,1,256]{2,1,0:T(1,128)S(1)} all-to-all(f32[32,1,256]{2,1,0:T(1,128)S(1)} %bitcast.9), channel_id=1, replica_groups=mesh['grp'=2,'tile'=16] {'grp','tile'}, dimensions={0} | all-to-all | bytes 65536 | tf_op jit(solution)/shard_map/all_to_all | solution.py:429
  35.0 1.3 %shard_map.40 = f32[32,512]{1,0:T(8,128)} custom-call(f32[64,128]{1,0:T(8,128)S(1)} %bitcast.8, f32[48,640]{1,0:T(8,128)S(1)} %get-tuple-element.23.rhs_ref, f32[48,640]{1,0:T(8,128)S(1)} %get-tuple-element.24.diag_ref, f32[48,640]{1,0:T(8,128)S(1)} %get-tuple-element.25.weight_ref, f32[48,640]{1,0:T(8,128)S(1)} %get-tuple-element.26.smooth_ref), custom_call_target="tpu_custom_call" | custom-call | tf_op jit(solution)/shard_map/pallas_call | solution.py:475
Async XLA Ops:
  1.2 14.8 %collective-permute-start = (f32[72,2048]{1,0:T(8,128)S(1)}, f32[72,2048]{1,0:T(8,128)S(1)}, u32[]{:S(2)}, u32[]{:S(2)}) collective-permute-start(f32[72,2048]{1,0:T(8,128)S(1)} %get-tuple-element.19.mine_ref), channel_id=1, source_target_pairs={{0,16},{16,0},{1,17},{17,1},{2,18},{18,2},{3,19},{19,3},{4,20},{20... | collective-permute-start | bytes 1769480 | tf_op jit(solution)/shard_map/ppermute | solution.py:449

commit v8 on v7

--- a/solution.py
+++ b/solution.py
@@ -83,6 +83,32 @@
     )
     mine = lax.rem(row_iota(line.shape), used) == lax.rem(lane_iota(line.shape) // per_row, used)
     line = jnp.where(mine, line, 0.0)
+    return jnp.sum(line, axis=0, keepdims=True) * (1.0 / (FAC * FAC))
+
+
+def block_means_of(x):
+    rows, cols = x.shape
+    per_row = cols // FAC
+    parts = []
+    for _ in range(3):
+        part = x.astype(jnp.bfloat16)
+        parts.append(part)
+        x = x - part.astype(jnp.float32)
+    pick = (
+        lax.broadcasted_iota(jnp.int32, (cols, LANES), 0) // FAC
+        == lax.rem(lane_iota((cols, LANES)), per_row)
+    )
+    out = jnp.dot(
+        jnp.concatenate(parts, axis=0),
+        pick.astype(jnp.bfloat16),
+        preferred_element_type=jnp.float32,
+    )
+    out = out[:rows] + out[rows : 2 * rows] + out[2 * rows :]
+    used = rows // FAC
+    mine = lax.rem(lane_iota((FAC, LANES)) // per_row, used)
+    line = out[:FAC]
+    for a in range(1, used):
+        line = jnp.where(mine == a, out[a * FAC : (a + 1) * FAC], line)
     return jnp.sum(line, axis=0, keepdims=True) * (1.0 / (FAC * FAC))
 
 
@@ -247,7 +273,7 @@
         smooth = (1.0 - OMEGA) * smooth + weight * (rhs + neighbour_sum(smooth))
     smooth_out[...] = smooth
     left_over = (rhs - (6.0 + diag) * smooth + neighbour_sum(smooth))[:rows, :cols]
-    coarse = block_means([left_over])
+    coarse = block_means_of(left_over)
     per_group = coarse_grid.per_group
     at = (g // 2) * tiles + t
     devices = LANES // here
@@ -371,12 +397,14 @@
     return gather_lanes(jnp.broadcast_to(line, shape), index)
 
 
-def last_kernel(grid, got_ref, rhs_ref, diag_ref, weight_ref, smooth_ref, out_ref, field_ref):
+def last_kernel(grid, got_ref, rhs_ref, diag_ref, weight_ref, smooth_ref, out_ref):
     rows, cols = out_ref.shape
     block_rows, per_row, per_tile = rows // FAC, cols // FAC, LANES // FAC
     here = block_rows * per_row
-    inside = inside_mask(grid, rows, cols)
     shape = (SUB, LANES)
+    lane = lane_iota(shape)
+    g, t = lax.axis_index("grp"), lax.axis_index("tile")
+    in_side = ((lane < HALO) & (t < grid[1] - 1)) | ((lane >= LANES - HALO) & (t > 0))
     total = got_ref[:SUB, :]
     for at in range(SUB, got_ref.shape[0], SUB):
         total = total + got_ref[at : at + SUB, :]
@@ -387,17 +415,19 @@
     def pick(line, at):
         return gather_lanes(jnp.broadcast_to(line, shape), jnp.full(shape, at, jnp.int32))
 
-    bands = [(a * FAC, FAC, second, here + a * per_row, here + a * per_row) for a in range(block_rows)]
-    bands += [(rows, HALO, ring, per_row, here + per_row), (rows + HALO, HALO, ring, 0, here)]
-    for start, height, line, at, side in bands:
+    def band(line, at, side, step):
         parts = [prolong_line(line, at + q * per_tile, shape) for q in range(cols // LANES)]
-        step = 0 if start < rows else 1
         beside, other = pick(ring, side + per_row - 1 - step), pick(ring, side + step)
-        parts.append(jnp.where(lane_iota(shape) < LANES // 2, beside, other))
-        for low in range(start, start + height, SUB):
-            for q, part in enumerate(parts):
-                field_ref[low : low + SUB, q * LANES : (q + 1) * LANES] = part
-    field = jnp.where(inside, smooth_ref[...] + MIX * field_ref[...], 0.0)
+        return parts + [jnp.where(in_side, jnp.where(lane < LANES // 2, beside, other), 0.0)]
+
+    bands = [band(second, here + a * per_row, here + a * per_row, 0) for a in range(block_rows)]
+    under = [jnp.where(g < grid[0] - 1, x, 0.0) for x in band(ring, per_row, here + per_row, 1)]
+    over = [jnp.where(g > 0, x, 0.0) for x in band(ring, 0, here, 1)]
+    tiles = [bands[at // FAC] for at in range(0, rows, SUB)] + [under, over]
+    field = jnp.concatenate(
+        [jnp.concatenate([tile[q] for tile in tiles], axis=0) for q in range(len(over))], axis=1
+    )
+    field = smooth_ref[...] + MIX * field
     rhs = rhs_ref[...]
     weight = weight_ref[...]
     rest = rhs - (6.0 + diag_ref[...]) * field + neighbour_sum(field)
@@ -473,7 +503,7 @@
     )(got, mine, theirs, term, ring)
     got = exchange(slots)
     (field,) = call(
-        points, functools.partial(last_kernel, grid), [(rows, cols)], 5, [wide]
+        points, functools.partial(last_kernel, grid), [(rows, cols)], 5
     )(got, rhs, diag, weight, smooth)
     return field
 

time: 36.5 us -> 36.5 us (level)
  no operation moved by 1% of the time
where the time goes in v8:
time: 36.5 us; the launch traced here: 36.3 us
  blocking collectives  32.1 us (88%)
  Pallas kernels  3.63 us (10%)
  starting transfers between devices  0.56 us (2%)
    all_to_all x3, blocking collectives, exchange(): lax.all_to_all(slots.reshape(count, lines * LANES), everyone, 0, 0, tiled...  32.1 us
    pallas_call x1, Pallas kernels, shards(): call(points, functools.partial(last_kernel, grid), [(rows, cols)], 5)  1.27 us
    pallas_call x1, Pallas kernels, shards(): pl.pallas_call(functools.partial(start_kernel, grid), out_shape=[jax.Shap...  1.14 us
    pallas_call x1, Pallas kernels, shards(): call(points, functools.partial(middle_kernel, grid, width), [wide] * 4 +...  0.91 us
  transfers between devices with their start and end apart: 1, of which 0 were waited for; matrix products, arithmetic and copies ran while one was open for 0% of the time, Pallas kernels for 0%

profile of v8, /device:TPU:0, one launch (start us, length us, event | category | flops | bytes accessed | tf_op | source)
XLA Modules:
  0.0 36.3 jit_solution(2495100427755602827)
XLA Ops:
  0.0 1.1 %shard_map.37 = (f32[160,128]{1,0:T(8,128)S(1)}, f32[32,512]{1,0:T(8,128)S(1)}, f32[32,512]{1,0:T(8,128)S(1)}, f32[72,2048]{1,0:T(8,128)S(1)}) custom-call(f32[32,512]{1,0:T(8,128)} %rhs_in.1, f32[32,512]{1,0:T(8,128)} %diag_in.1, f32[64,2048]{1,0:T(8,128)} %factor_in.1), custom_call_target="tpu_custom_call" | custom-call | tf_op jit(solution)/shard_map/pallas_call | solution.py:466
  1.2 0.6 %collective-permute-start = (f32[72,2048]{1,0:T(8,128)S(1)}, f32[72,2048]{1,0:T(8,128)S(1)}, u32[]{:S(2)}, u32[]{:S(2)}) collective-permute-start(f32[72,2048]{1,0:T(8,128)S(1)} %get-tuple-element.19.mine_ref), channel_id=1, source_target_pairs={{0,16},{16,0},{1,17},{17,1},{2,18},{18,2},{3,19},{19,3},{4,20},{20... | collective-permute-start | bytes 1769480 | tf_op jit(solution)/shard_map/ppermute | solution.py:479
  1.7 14.2 %all_to_all.27 = f32[32,1,640]{2,1,0:T(1,128)S(1)} all-to-all(f32[32,1,640]{2,1,0:T(1,128)S(1)} %bitcast.10), channel_id=1, replica_groups=mesh['grp'=2,'tile'=16] {'grp','tile'}, dimensions={0} | all-to-all | bytes 163840 | tf_op jit(solution)/shard_map/all_to_all | solution.py:459
  15.9 0.0 collective-permute-done.theirs_ref
  15.9 0.9 %shard_map.38 = (f32[48,640]{1,0:T(8,128)S(1)}, f32[48,640]{1,0:T(8,128)S(1)}, f32[48,640]{1,0:T(8,128)S(1)}, f32[48,640]{1,0:T(8,128)S(1)}, f32[2,16,128]{2,1,0...) custom-call(f32[160,128]{1,0:T(8,128)S(1)} %bitcast.6, f32[32,512]{1,0:T(8,128)S(1)} %get-tuple-element.17.rhs_ref, ...), custom_call_target="tpu_custom_call" | custom-call | tf_op jit(solution)/shard_map/pallas_call | solution.py:488
  16.8 9.0 %all_to_all.28 = f32[32,1,512]{2,1,0:T(1,128)S(1)} all-to-all(f32[32,1,512]{2,1,0:T(1,128)S(1)} %bitcast.11), channel_id=1, replica_groups=mesh['grp'=2,'tile'=16] {'grp','tile'}, dimensions={0} | all-to-all | bytes 131072 | tf_op jit(solution)/shard_map/all_to_all | solution.py:459
  25.8 0.3 shard_map.39
  26.1 8.9 %all_to_all.29 = f32[32,1,256]{2,1,0:T(1,128)S(1)} all-to-all(f32[32,1,256]{2,1,0:T(1,128)S(1)} %bitcast.9), channel_id=1, replica_groups=mesh['grp'=2,'tile'=16] {'grp','tile'}, dimensions={0} | all-to-all | bytes 65536 | tf_op jit(solution)/shard_map/all_to_all | solution.py:459
  35.0 1.3 %shard_map.40 = f32[32,512]{1,0:T(8,128)} custom-call(f32[64,128]{1,0:T(8,128)S(1)} %bitcast.8, f32[48,640]{1,0:T(8,128)S(1)} %get-tuple-element.23.rhs_ref, f32[48,640]{1,0:T(8,128)S(1)} %get-tuple-element.24.diag_ref, f32[48,640]{1,0:T(8,128)S(1)} %get-tuple-element.25.weight_ref, f32[48,640]{1,0:T(8,128)S(1)} %get-tuple-element.26.smooth_ref), custom_call_target="tpu_custom_call" | custom-call | tf_op jit(solution)/shard_map/pallas_call | solution.py:505
Async XLA Ops:
  1.2 14.8 %collective-permute-start = (f32[72,2048]{1,0:T(8,128)S(1)}, f32[72,2048]{1,0:T(8,128)S(1)}, u32[]{:S(2)}, u32[]{:S(2)}) collective-permute-start(f32[72,2048]{1,0:T(8,128)S(1)} %get-tuple-element.19.mine_ref), channel_id=1, source_target_pairs={{0,16},{16,0},{1,17},{17,1},{2,18},{18,2},{3,19},{19,3},{4,20},{20... | collective-permute-start | bytes 1769480 | tf_op jit(solution)/shard_map/ppermute | solution.py:479
